TPU v7x, 32 devices: a whole 2x2x4 slice. The times are simulated.
32 devices in a mesh: groups: 2 (over x), seq: 16 (over z, y, core).
Axes of the slice: x: 2, y: 2, z: 4, core: 2. Of those that a mesh axis runs over, the one named last changes fastest.
Arguments:
- queries: bfloat16 [4096, 2048], P(('groups', 'seq')), parts along dimension 0, may hold values from -140 to 140
- keys: bfloat16 [4096, 2048], P(('groups', 'seq')), parts along dimension 0, may hold values from -6.25 to 6.25
- values: bfloat16 [4096, 2048], P(('groups', 'seq')), parts along dimension 0, may hold values from -6 to 6
- grad_out: bfloat16 [4096, 2048], P(('groups', 'seq')), parts along dimension 0, may hold values from -6 to 6
- partners: int32 [32, 16, 3], P(('groups', 'seq')), parts along dimension 0, may hold values from 0 to 15, all different within a row; in each aligned block of 16 rows (0 to 15, 16 to 31, ..., all dimensions but the last counted through in order) at most 3 rows name the same one
Outputs:
- grad_queries: bfloat16 [4096, 2048], P(('groups', 'seq')), parts along dimension 0
- grad_keys: bfloat16 [4096, 2048], P(('groups', 'seq')), parts along dimension 0
- grad_values: bfloat16 [4096, 2048], P(('groups', 'seq')), parts along dimension 0
There are 2 independent parts, one for each index of `groups`. A program takes and returns all parts, laid end to end along the dimension named above; each array names one. Nothing has to cross between parts.
Inputs may be any that keep to these rules, and one draw needn't show every extreme that they name: In the 16 head rows of one query block, no block is named more than 3 times, and some block is named exactly 3 times; the 3 partners of one head are different blocks.
All inputs are finite; a program needn't handle non-finite values.
Results may differ from a plain program's by a relative error of at most 0.01.
Values may be sent and summed in bfloat16 or wider, within the bound.
A program may use at most 128 MiB of HBM per device.

v0:
```python
import math

import jax
import jax.numpy as jnp
from jax import lax
from jax.sharding import PartitionSpec as P

H = 16
HD = 128


def with_halo(shard, sides, width):
    for axis, dim in sides:
        count, length = (lax.axis_size(axis), shard.shape[dim])
        up = [(i, (i + 1) % count) for i in range(count - 1)]
        down = [(j, i) for i, j in up]
        last = lax.slice_in_dim(shard, length - width, length, axis=dim)
        first = lax.slice_in_dim(shard, 0, width, axis=dim)
        before = lax.ppermute(last, axis, up)
        after = lax.ppermute(first, axis, down)
        shard = jnp.concatenate([before, shard, after], axis=dim)
    return shard


def broadcast(block, axis, source):
    block = jnp.where(lax.axis_index(axis) == source, block, jnp.zeros_like(block))
    return lax.psum(block, axis)


def per_device(queries, keys, values, grad_out, partners):
    devices = lax.axis_size("seq")
    my_index = lax.axis_index("seq")
    most_slots = max(2, (3 * H + devices - 1) // devices)
    softmax_scale = 1.0 / math.sqrt(HD)
    width = H * HD
    rows_here = queries.shape[0]
    kv_local = jnp.stack([keys, values])
    query_heads = queries.reshape(rows_here, H, HD)
    grad_heads = grad_out.reshape(rows_here, H, HD)
    lower_ok = my_index > 0
    upper_ok = my_index < devices - 1
    window = with_halo(kv_local, (("seq", 1),), rows_here)
    sink_parts = [broadcast(kv_local, "seq", sink_root) for sink_root in range(2)]
    near_kv = jnp.concatenate([window] + sink_parts, axis=1).reshape(2, 5 * rows_here, H, HD)
    near_keys = near_kv[0]
    near_values = near_kv[1]
    item_count = 3 * H
    dests = partners.reshape(item_count)
    item_heads = jnp.arange(item_count, dtype=jnp.int32) // 3
    dest_hot = (dests[:, None] == jnp.arange(devices, dtype=jnp.int32)[None, :]).astype(jnp.int32)
    slot_rank = jnp.sum((jnp.cumsum(dest_hot, axis=0) - dest_hot) * dest_hot, axis=1)
    kv_by_head = kv_local.reshape(2, rows_here, H, HD).transpose(2, 0, 1, 3)
    requests = jnp.full((devices, most_slots), -1, jnp.int32).at[dests, slot_rank].set(item_heads)
    wanted = lax.all_to_all(requests, "seq", split_axis=0, concat_axis=0, tiled=True)
    picked = kv_by_head[jnp.maximum(wanted, 0)]
    fetched = lax.all_to_all(
        jnp.where((wanted >= 0)[:, :, None, None, None], picked, jnp.zeros_like(picked)),
        "seq",
        split_axis=0,
        concat_axis=0,
        tiled=True,
    )
    far_kv = fetched[dests, slot_rank].reshape(H, 3, 2, rows_here, HD)
    far_keys = far_kv[:, :, 0]
    far_values = far_kv[:, :, 1]
    near_scores = softmax_scale * jnp.einsum(
        "thd,khd->htk", query_heads, near_keys, preferred_element_type=jnp.float32
    )
    far_scores = softmax_scale * jnp.einsum(
        "thd,hrkd->htrk", query_heads, far_keys, preferred_element_type=jnp.float32
    )
    key_pos = jnp.arange(5 * rows_here, dtype=jnp.int32)
    key_ok = jnp.logical_not((key_pos < rows_here) & jnp.logical_not(lower_ok))
    key_ok = key_ok & jnp.logical_not(
        (key_pos >= 2 * rows_here) & (key_pos < 3 * rows_here) & jnp.logical_not(upper_ok)
    )
    near_max = jnp.max(
        jnp.where(key_ok[None, None, :], near_scores, -jnp.inf), axis=2, keepdims=True
    )
    far_max = jnp.max(far_scores, axis=(2, 3))[:, :, None]
    row_max = jnp.maximum(near_max, far_max)
    near_total = jnp.sum(
        jnp.where(key_ok[None, None, :], jnp.exp(near_scores - row_max), 0.0), axis=2, keepdims=True
    )
    far_total = jnp.sum(jnp.exp(far_scores - row_max[:, :, :, None]), axis=(2, 3))[:, :, None]
    totals = near_total + far_total

    def near_prob_f32():
        return jnp.where(key_ok[None, None, :], jnp.exp(near_scores - row_max), 0.0) / totals

    def far_prob_f32():
        return jnp.exp(far_scores - row_max[:, :, :, None]) / totals[:, :, :, None]

    near_probs = near_prob_f32().astype(jnp.bfloat16)
    far_probs = far_prob_f32().astype(jnp.bfloat16)
    attended = jnp.einsum(
        "htk,khd->htd", near_probs, near_values, preferred_element_type=jnp.float32
    )
    attended = attended + jnp.einsum(
        "htrk,hrkd->htd", far_probs, far_values, preferred_element_type=jnp.float32
    )
    delta = jnp.sum(grad_heads.transpose(1, 0, 2) * attended, axis=2)
    near_dprob = jnp.einsum(
        "thd,khd->htk", grad_heads, near_values, preferred_element_type=jnp.float32
    )
    far_dprob = jnp.einsum(
        "thd,hrkd->htrk", grad_heads, far_values, preferred_element_type=jnp.float32
    )
    near_dscore = (near_prob_f32() * (near_dprob - delta[:, :, None])).astype(jnp.bfloat16)
    far_dscore = (far_prob_f32() * (far_dprob - delta[:, :, None, None])).astype(jnp.bfloat16)
    grad_q = jnp.einsum("htk,khd->thd", near_dscore, near_keys, preferred_element_type=jnp.float32)
    grad_q = grad_q + jnp.einsum(
        "htrk,hrkd->thd", far_dscore, far_keys, preferred_element_type=jnp.float32
    )
    grad_queries = (softmax_scale * grad_q).reshape(rows_here, width).astype(jnp.bfloat16)
    near_key_term = softmax_scale * jnp.einsum(
        "htk,thd->khd", near_dscore, query_heads, preferred_element_type=jnp.float32
    )
    near_value_term = jnp.einsum(
        "htk,thd->khd", near_probs, grad_heads, preferred_element_type=jnp.float32
    )
    near_terms = jnp.stack(
        [near_key_term.reshape(5 * rows_here, width), near_value_term.reshape(5 * rows_here, width)]
    )
    own_grads = near_terms[:, rows_here : 2 * rows_here]
    outgoing = jnp.concatenate(
        [near_terms[:, :rows_here], near_terms[:, 2 * rows_here : 3 * rows_here]], axis=1
    )
    incoming = with_halo(outgoing.astype(jnp.bfloat16), (("seq", 1),), rows_here).astype(
        outgoing.dtype
    )
    own_grads = own_grads + incoming[:, :rows_here] + incoming[:, 3 * rows_here :]
    sink_terms = (
        near_terms[:, 3 * rows_here :].reshape(2, 2, rows_here, width).transpose(1, 0, 2, 3)
    )
    sink_total = lax.psum(sink_terms, "seq")
    sink_mine = lax.dynamic_index_in_dim(sink_total, jnp.minimum(my_index, 1), 0, keepdims=False)
    own_grads = own_grads + jnp.where(my_index < 2, sink_mine, jnp.zeros_like(sink_mine))
    far_key_term = softmax_scale * jnp.einsum(
        "htrk,thd->hrkd", far_dscore, query_heads, preferred_element_type=jnp.float32
    )
    far_value_term = jnp.einsum(
        "htrk,thd->hrkd", far_probs, grad_heads, preferred_element_type=jnp.float32
    )
    far_terms = (
        jnp.stack([far_key_term, far_value_term], axis=2)
        .astype(jnp.bfloat16)
        .reshape(item_count, 2, rows_here, HD)
    )
    outbox = (
        jnp.zeros((devices, most_slots, 2, rows_here, HD), jnp.bfloat16)
        .at[dests, slot_rank]
        .set(far_terms)
    )
    returned = lax.all_to_all(outbox, "seq", split_axis=0, concat_axis=0, tiled=True)
    head_hot = (wanted[:, :, None] == jnp.arange(H, dtype=jnp.int32)[None, None, :]).astype(
        jnp.bfloat16
    )
    gained = jnp.einsum("nmh,nmcbd->cbhd", head_hot, returned, preferred_element_type=jnp.float32)
    own_grads = own_grads + gained.reshape(2, rows_here, width)
    return (grad_queries, own_grads[0].astype(jnp.bfloat16), own_grads[1].astype(jnp.bfloat16))


def solution(mesh):
    placed = (
        P(("groups", "seq"), None),
        P(("groups", "seq"), None),
        P(("groups", "seq"), None),
        P(("groups", "seq"), None),
        P(("groups", "seq"), None, None),
    )
    return jax.shard_map(
        per_device,
        mesh=mesh,
        in_specs=placed,
        out_specs=(
            P(("groups", "seq"), None),
            P(("groups", "seq"), None),
            P(("groups", "seq"), None),
        ),
        check_vma=False,
    )
```

profile of v0, /device:TPU:0, one launch (start us, length us, event | category | flops | bytes accessed | tf_op | source)
XLA Modules:
  0.0 458.9 jit_solution(7758403241742781614)
XLA Ops:
  8.5 2.8 scatter_fusion
  12.0 7.4 %all-to-all-start = ((s32[16,1,3]{2,1,0:T(1,128)}), s32[16,1,3]{2,1,0:T(1,128)S(1)}, u32[]{:S(2)}, u32[]{:S(2)}) async-start(s32[16,1,3]{2,1,0:T(1,128)} %copy.159), calls=%async_computation | async-start | bytes 16384 | tf_op jit(solution)/shard_map/all_to_all | solution.py:54
  19.4 1.3 copy.154
  21.7 4.0 all-to-all-done
  26.0 2.7 gather_fusion
  28.7 3.8 broadcast_select_fusion
  32.5 4.5 all-to-all-start.1
  37.2 2.2 collective-permute-start
  39.4 1.5 collective-permute-start.1
  41.8 2.0 broadcast_select_fusion.1
  43.8 2.3 copy-done.6
  47.3 1.2 copy.179
  48.5 2.4 constant_dynamic-update-slice_fusion.2
  50.9 169.4 %all-reduce.6.cloned.1.call-done = (bf16[2,128,2048]{1,2,0:T(8,128)(2,1)}, bf16[2,128,2048]{1,2,0:T(8,128)(2,1)}) async-done(((bf16[2,128,2048]{1,2,0:T(8,128)(2,1)}, bf16[2,128,2048]{1,2,0:T(8,128)(2,1)}), (bf16[2,128,2048]{1,2,0:T(8,128)(2,1)}, bf16[2,128,2048]{1,2,0:T(8,128)(2,1)})) %all-reduce.6.cloned.1.call-update) | async-done | bytes 2097168 | tf_op jit(solution)/shard_map/psum | solution.py:27
  220.3 2.4 constant_dynamic-update-slice_fusion.1
  222.7 2.3 constant_dynamic-update-slice_fusion
  225.0 4.6 %fusion.52 = (bf16[1,640,2048]{1,2,0:T(8,128)(2,1)}, bf16[1,640,2048]{1,2,0:T(8,128)(2,1)S(1)}) fusion(bf16[2,640,2048]{1,2,0:T(8,128)(2,1)} %constant_dynamic-update-slice_fusion), kind=kLoop, calls=%fused_computation.102 | loop fusion | bytes 10485760 | tf_op jit(solution)/shard_map/slice | solution.py:46
  229.6 3.7 select_reduce_fusion
  233.3 4.7 %gather_fusion.1 = bf16[48,2,128,128]{3,2,1,0:T(8,128)(2,1)} fusion(bf16[16,3,2,128,128]{4,3,2,1,0:T(8,128)(2,1)} %all-to-all-done.1, s32[48]{0:T(128)S(1)} %bitcast.171), kind=kCustom, calls=%fused_computation.1 | custom fusion | bytes 6291840 | tf_op jit(solution)/shard_map/gather | solution.py:63
  238.0 2.1 copy.166
  240.7 3.0 copy-done.2
  243.7 1.1 bitcast_reduce_fusion
  245.4 1.1 fusion.21
  248.2 1.8 fusion.29
  252.2 2.2 pad_maximum_fusion.1
  254.3 2.5 broadcast.125
  256.9 9.6 %scatter_fusion.1 = bf16[16,3,2,128,128]{4,3,2,1,0:T(8,128)(2,1)} fusion(bf16[16,3,2,128,128]{4,3,2,1,0:T(8,128)(2,1)} %broadcast.125, s32[48]{0:T(128)S(1)} %get-tuple-element.20, bf16[48,2,128,128]{3,2,1,0:T(8,128)(2,1)} %pad_maximum_fusion.1), kind=kCustom, calls=%fused_computation.3 | custom fusion | bytes 9437568 | tf_op jit(solution)/shard_map/scatter | solution.py:153
  266.4 4.5 all-to-all-start.2
  271.0 5.7 %fusion.1 = bf16[16,128,640]{1,2,0:T(8,128)(2,1)S(1)} fusion(f32[16,128]{1,0:T(8,128)S(1)} %fusion.29, bf16[640,16,128]{0,2,1:T(8,128)(2,1)} %bitcast.167, bf16[128,16,128]{0,2,1:T(8,128)(2,1)} %bitcast.173, f32[16,128]{1,0:T(8,128)S(1)} %add.70, f32[16,128]{1,0:T(8,128)S(1)} %max.27, f32[16,640,128]{2,1,0:T(8,128)} %get-tuple-element.32, ...), kind=kOutput, calls=%fused_computation.11 | convolution fusion | flops 344719360 | bytes 11035264 | tf_op jit(solution)/shard_map/thd,khd->htk/dot_general | solution.py:103
  276.7 1.6 copy-done.4
  278.3 3.2 multiply_bitcast_fusion
  281.5 6.0 %copy.181 = f32[640,16,128]{0,2,1:T(8,128)} copy(f32[640,16,128]{2,0,1:T(8,128)} %multiply_bitcast_fusion) | data formatting | bytes 10485760 | tf_op jit(solution)/shard_map/mul | solution.py:116
  287.5 4.1 fusion.25
  291.6 2.3 copy-done.1
  293.9 2.3 fusion.2
  296.2 5.4 %copy.183 = f32[2,256,2048]{2,1,0:T(8,128)} copy(f32[2,256,2048]{1,2,0:T(8,128)} %fusion.2) | data formatting | bytes 8388608 | tf_op jit(solution)/shard_map/slice | solution.py:134
  301.6 5.3 %copy.184 = f32[2,2,128,2048]{2,3,0,1:T(8,128)} copy(f32[2,2,128,2048]{3,2,1,0:T(8,128)} %bitcast.151) | data formatting | bytes 8388608 | tf_op jit(solution)/shard_map/reshape | solution.py:134
  307.0 4.8 %fusion = bf16[2,640,2048]{1,2,0:T(8,128)(2,1)S(1)} fusion(f32[1,640,2048]{1,2,0:T(8,128)} %bitcast.146, f32[1,640,2048]{1,2,0:T(8,128)} %bitcast.142), kind=kLoop, calls=%fused_computation.9 | loop fusion | flops 2621440 | bytes 15728640 | tf_op jit(solution)/shard_map/convert.9
  311.8 1.7 fusion.51
  313.5 1.3 collective-permute-start.3
  314.7 4.0 collective-permute-start.2
  318.7 2.8 fusion.22
  322.5 1.0 copy.191
  323.5 14.6 %all-to-all-done.2 = bf16[16,3,2,128,128]{4,3,2,1,0:T(8,128)(2,1)} async-done(((bf16[16,3,2,128,128]{4,3,2,1,0:T(8,128)(2,1)}), bf16[16,3,2,128,128]{4,3,2,1,0:T(8,128)(2,1)}, u32[]{:S(2)}, u32[]{:S(2)}) %all-to-all-start.2) | async-done | bytes 3145760 | tf_op jit(solution)/shard_map/all_to_all | solution.py:155
  338.0 5.0 %fusion.15 = f32[2,128,16,128]{3,2,1,0:T(8,128)} fusion(bf16[16,3,2,128,128]{4,3,2,1,0:T(8,128)(2,1)} %all-to-all-done.2, s32[16,3]{0,1:T(4,128)S(1)} %bitcast.178), kind=kOutput, calls=%fused_computation.37 | convolution fusion | flops 50332416 | bytes 5243072 | tf_op jit(solution)/shard_map/nmh,nmcbd->cbhd/dot_general | solution.py:159
  343.0 2.0 copy.222
  345.1 101.8 %all-reduce.4.cloned.1.call-done = f32[2,2,128,2048]{2,3,1,0:T(8,128)} async-done(((f32[2,2,128,2048]{2,3,1,0:T(8,128)}), f32[2,2,128,2048]{2,3,1,0:T(8,128)}) %all-reduce.4.cloned.1.call-update) | async-done | bytes 4194320 | tf_op jit(solution)/shard_map/psum | solution.py:136
  446.8 3.2 fusion.14
  (73 shorter events, 13.6 us)
Async XLA Ops:
  7.2 13.8 %copy-start.11 = (bf16[128,2048]{1,0:T(8,128)(2,1)S(1)}, bf16[128,2048]{1,0:T(8,128)(2,1)}, u32[]{:S(2)}) copy-start(bf16[128,2048]{1,0:T(8,128)(2,1)} %param.6) | copy-start | bytes 1572868
  12.0 13.7 %all-to-all-start = ((s32[16,1,3]{2,1,0:T(1,128)}), s32[16,1,3]{2,1,0:T(1,128)S(1)}, u32[]{:S(2)}, u32[]{:S(2)}) async-start(s32[16,1,3]{2,1,0:T(1,128)} %copy.159), calls=%async_computation | async-start | bytes 16384 | tf_op jit(solution)/shard_map/all_to_all | solution.py:54
  32.5 200.8 %all-to-all-start.1 = ((bf16[16,3,2,128,128]{4,3,2,1,0:T(8,128)(2,1)}), bf16[16,3,2,128,128]{4,3,2,1,0:T(8,128)(2,1)}, u32[]{:S(2)}, u32[]{:S(2)}) async-start(bf16[16,3,2,128,128]{4,3,2,1,0:T(8,128)(2,1)} %broadcast_select_fusion), calls=%async_computation.1 | async-start | bytes 6291456 | tf_op jit(solution)/shard_map/all_to_all | solution.py:56
  37.0 183.3 %all-reduce.6.cloned.1.call-start = ((), (), s32[]{:S(2)}) async-start(), calls=%async_computation.4 | async-start | bytes 4194304 | tf_op jit(solution)/shard_map/psum | solution.py:27
  37.2 4.4 collective-permute-start
  39.4 9.1 %collective-permute-start.1 = (bf16[2,128,2048]{1,2,0:T(8,128)(2,1)S(1)}, bf16[2,128,2048]{1,2,0:T(8,128)(2,1)}, u32[]{:S(2)}, u32[]{:S(2)}) collective-permute-start(bf16[2,128,2048]{1,2,0:T(8,128)(2,1)S(1)} %pad_maximum_fusion.5), channel_id=1, source_target_pairs={{1,0},{2,1},{3,2},{4,3},{5,4},{6,5},{7,6},{8,7},{9,8},{10,9},{11,1... | collective-permute-start | bytes 3145736 | tf_op jit(solution)/shard_map/ppermute | solution.py:20
  41.8 4.3 copy-start.12
  43.8 2.3 copy-start.6
  46.1 1.0 copy-start.13
  225.0 4.6 %copy-start.8 = (bf16[128,16,128]{0,2,1:T(8,128)(2,1)S(1)}, bf16[128,16,128]{0,2,1:T(8,128)(2,1)}, u32[]{:S(2)}) copy-start(bf16[128,16,128]{0,2,1:T(8,128)(2,1)} %copy.179) | copy-start | bytes 1572868
  240.1 10.0 %copy-start.3 = (bf16[48,2,128,128]{3,2,0,1:T(8,128)(2,1)}, bf16[48,2,128,128]{3,2,0,1:T(8,128)(2,1)S(1)}, u32[]{:S(2)}) copy-start(bf16[48,2,128,128]{3,2,0,1:T(8,128)(2,1)S(1)} %copy.166) | copy-start | bytes 9437188
  240.1 3.6 copy-start.2
  245.4 1.1 copy-start.14
  246.5 1.7 copy-start.10
  251.0 1.1 copy-start.7
  266.4 71.6 %all-to-all-start.2 = ((bf16[16,3,2,128,128]{4,3,2,1,0:T(8,128)(2,1)}), bf16[16,3,2,128,128]{4,3,2,1,0:T(8,128)(2,1)}, u32[]{:S(2)}, u32[]{:S(2)}) async-start(bf16[16,3,2,128,128]{4,3,2,1,0:T(8,128)(2,1)} %scatter_fusion.1), calls=%async_computation.2 | async-start | bytes 6291456 | tf_op jit(solution)/shard_map/all_to_all | solution.py:155
  270.9 7.4 %copy-start.9 = (bf16[128,16,128]{0,2,1:T(8,128)(2,1)S(1)}, bf16[128,16,128]{0,2,1:T(8,128)(2,1)}, u32[]{:S(2)}) copy-start(bf16[128,16,128]{0,2,1:T(8,128)(2,1)} %copy.179) | copy-start | bytes 1572868
  270.9 175.9 %all-reduce.4.cloned.1.call-start = ((), (), s32[]{:S(2)}) async-start(), calls=%async_computation.3 | async-start | bytes 8388608 | tf_op jit(solution)/shard_map/psum | solution.py:136
  276.7 1.6 copy-start.4
  281.5 6.0 %copy-start.15 = (bf16[128,2048]{0,1:T(8,128)(2,1)S(1)}, bf16[128,2048]{0,1:T(8,128)(2,1)}, u32[]{:S(2)}) copy-start(bf16[128,2048]{0,1:T(8,128)(2,1)} %copy.168) | copy-start | bytes 1572868
  287.5 6.5 %copy-start = (f32[640,16,128]{0,2,1:T(8,128)S(1)}, f32[640,16,128]{0,2,1:T(8,128)}, u32[]{:S(2)}) copy-start(f32[640,16,128]{0,2,1:T(8,128)} %copy.181) | copy-start | bytes 15728644
  291.6 2.3 copy-start.1
  313.5 31.6 %collective-permute-start.3 = (bf16[2,128,2048]{1,2,0:T(8,128)(2,1)}, bf16[2,128,2048]{1,2,0:T(8,128)(2,1)}, u32[]{:S(2)}, u32[]{:S(2)}) collective-permute-start(bf16[2,128,2048]{1,2,0:T(8,128)(2,1)} %get-tuple-element.23), channel_id=1, source_target_pairs={{1,0},{2,1},{3,2},{4,3},{5,4},{6,5},{7,6},{8,7},{9,8},{10,9},{11,1... | collective-permute-start | bytes 3145736 | tf_op jit(solution)/shard_map/ppermute | solution.py:20
  314.7 30.3 %collective-permute-start.2 = (bf16[2,128,2048]{1,2,0:T(8,128)(2,1)}, bf16[2,128,2048]{1,2,0:T(8,128)(2,1)}, u32[]{:S(2)}, u32[]{:S(2)}) collective-permute-start(bf16[2,128,2048]{1,2,0:T(8,128)(2,1)} %get-tuple-element.22), channel_id=1, source_target_pairs={{0,1},{1,2},{2,3},{3,4},{4,5},{5,6},{6,7},{7,8},{8,9},{9,10},{10,1... | collective-permute-start | bytes 3145736 | tf_op jit(solution)/shard_map/ppermute | solution.py:19
  318.7 2.8 copy-start.5
Sparse Core Ops, SparseCore 0:
  46.2 173.9 all-reduce.5
  307.1 139.6 all-reduce.3
where the time goes:
time: 460 us; the launch traced here: 459 us
  waiting for transfers between devices  291 us (63%)
  local copies, waits for them, and re-layouts  77 us (17%)
  matrix products  31.2 us (7%)
  starting transfers between devices  25.4 us (6%)
  other arithmetic  20.4 us (4%)
  between operations  14.5 us (3%)
    psum x1, waiting for transfers between devices, broadcast(): return lax.psum(block, axis)  169 us
    psum x1, waiting for transfers between devices, per_device(): sink_total = lax.psum(sink_terms, 'seq')  102 us
    unnamed x43, local copies, waits for them, and re-layouts  22.3 us
    all_to_all x1, waiting for transfers between devices, per_device(): lax.all_to_all(outbox, 'seq', split_axis=0, concat_axis=0, tiled=True)  14.6 us
    scatter x1, local copies, waits for them, and re-layouts, per_device(): outbox = jnp.zeros((devices, most_slots, 2, rows_here, HD), jnp.bfloat16)...  9.59 us
  transfers between devices with their start and end apart: 9, of which 5 were waited for; matrix products, arithmetic and copies ran while one was open for 16% of the time, Pallas kernels for 0%

commit v1 on v0

v1 whole, which is shorter than its diff:
```python
import functools
import math

import jax
import jax.numpy as jnp
from jax import lax
from jax.experimental import pallas as pl
from jax.experimental.pallas import tpu as pltpu
from jax.sharding import PartitionSpec as P

H = 16
HD = 128
BLK = 128
WIDTH = H * HD
SCALE = 1.0 / math.sqrt(HD)
STRIDE = 4
CHUNKS = 8
ROWS = 2 * BLK // CHUNKS
ANY = pl.BlockSpec(memory_space=pl.ANY)
VMEM = pl.BlockSpec(memory_space=pltpu.VMEM)
SMEM = pl.BlockSpec(memory_space=pltpu.SMEM)


def remote(src, dst, send, recv, target):
    return pltpu.make_async_remote_copy(
        src_ref=src, dst_ref=dst, send_sem=send, recv_sem=recv,
        device_id={"seq": target}, device_id_type=pl.DeviceIdType.MESH,
    )


def relations(n):
    me = lax.axis_index("seq")
    return dict(
        me=me,
        core=lax.rem(me, 2),
        sibling=me + 1 - 2 * lax.rem(me, 2),
        lower=me > 0,
        upper=me < n - 1,
        root=me < 2,
        side=jnp.logical_and(me >= 2, me < 4),
        down=me >= STRIDE,
        up=me + STRIDE < n,
    )


def greet(r):
    me = r["me"]
    barrier = pltpu.get_barrier_semaphore()
    peers = ((r["lower"], -1), (r["upper"], 1), (r["down"], -STRIDE), (r["up"], STRIDE), (r["root"], 2), (r["side"], -2))
    for ok, step in peers:
        @pl.when(ok)
        def _(step=step):
            pl.semaphore_signal(barrier, inc=1, device_id={"seq": me + step}, device_id_type=pl.DeviceIdType.MESH)
    pl.semaphore_wait(barrier, sum(ok.astype(jnp.int32) for ok, _ in peers))


def piece(ref, lead, i):
    return ref.at[lead, i // (CHUNKS // 2), pl.ds((i % (CHUNKS // 2)) * ROWS, ROWS)]


def spread_kernel(n, keys, values, near, local, tree_s, tree_r, side_s, sib_s, sib_r, halo_s, halo_r):
    r = relations(n)
    me, core = r["me"], r["core"]
    greet(r)

    def own(i):
        ref = keys if i < CHUNKS // 2 else values
        return ref.at[pl.ds((i % (CHUNKS // 2)) * ROWS, ROWS)]

    def at_local(i):
        return pltpu.make_async_copy(own(i), piece(near, 2 + core, i), local.at[i])

    def to_up(i):
        return remote(piece(near, 2 + core, i), piece(near, 2 + core, i), tree_s.at[i], tree_r.at[i], me + STRIDE)

    def to_side(i):
        return remote(piece(near, 2 + core, i), piece(near, 2 + core, i), side_s.at[i], tree_r.at[i], me + 2)

    def to_sibling(i):
        return remote(piece(near, 2 + core, i), piece(near, 2 + core, i), sib_s.at[i], sib_r.at[i], r["sibling"])

    def from_sibling(i):
        return remote(piece(near, 3 - core, i), piece(near, 3 - core, i), sib_s.at[i], sib_r.at[i], r["sibling"])

    def to_halo(t, up):
        ref = (keys, values)[t]
        slot = 0 if up else 1
        return remote(ref, near.at[slot, t], halo_s.at[slot, t], halo_r.at[slot, t], me + (1 if up else -1))

    @pl.when(r["root"])
    def _():
        for i in range(CHUNKS):
            at_local(i).start()

    for t in range(2):
        for ok, up in ((r["upper"], True), (r["lower"], False)):
            @pl.when(ok)
            def _(t=t, up=up):
                to_halo(t, up).start()

    for i in range(CHUNKS):
        @pl.when(r["root"])
        def _(i=i):
            at_local(i).wait()

        @pl.when(jnp.logical_not(r["root"]))
        def _(i=i):
            to_up(i).wait_recv()

        @pl.when(r["up"])
        def _(i=i):
            to_up(i).start()

        @pl.when(r["root"])
        def _(i=i):
            to_side(i).start()

        to_sibling(i).start()

    for i in range(CHUNKS):
        from_sibling(i).wait_recv()
        to_sibling(i).wait_send()

        @pl.when(r["up"])
        def _(i=i):
            to_up(i).wait_send()

        @pl.when(r["root"])
        def _(i=i):
            to_side(i).wait_send()

    for t in range(2):
        for ok, up in ((r["upper"], True), (r["lower"], False)):
            @pl.when(ok)
            def _(t=t, up=up):
                to_halo(t, up).wait_send()
        for ok, up in ((r["lower"], True), (r["upper"], False)):
            @pl.when(ok)
            def _(t=t, up=up):
                to_halo(t, up).wait_recv()


def spread(keys, values, n):
    return pl.pallas_call(
        functools.partial(spread_kernel, n),
        out_shape=jax.ShapeDtypeStruct((4, 2, BLK, WIDTH), jnp.bfloat16),
        in_specs=[ANY, ANY],
        out_specs=ANY,
        scratch_shapes=[pltpu.SemaphoreType.DMA((CHUNKS,))] * 6
        + [pltpu.SemaphoreType.DMA((2, 2)), pltpu.SemaphoreType.DMA((2, 2))],
        compiler_params=pltpu.CompilerParams(
            collective_id=0, has_side_effects=True, vmem_limit_bytes=48 << 20),
        cost_estimate=pl.CostEstimate(flops=40_000_000_000, bytes_accessed=8 << 20, transcendentals=0),
        name="spread",
    )(keys, values)


def gather_kernel(n, window, sinks, halo, total, sib_in, tree_in, side_in, tree_out,
                  tree_s, tree_r, side_r, sib_s, sib_r, halo_s, halo_r):
    r = relations(n)
    me, core = r["me"], r["core"]
    greet(r)

    def to_sibling(i):
        return remote(piece(sinks, 1 - core, i), sib_in.at[i], sib_s.at[i], sib_r.at[i], r["sibling"])

    def to_down(i):
        return remote(tree_out.at[i], tree_in.at[i], tree_s.at[i], tree_r.at[i], me - STRIDE)

    def to_side(i):
        return remote(tree_out.at[i], side_in.at[i], tree_s.at[i], side_r.at[i], me - 2)

    def to_halo(t, up):
        return remote(window.at[1 if up else 0, t], halo.at[0 if up else 1, t],
                      halo_s.at[0 if up else 1, t], halo_r.at[0 if up else 1, t], me + (1 if up else -1))

    for i in range(CHUNKS):
        to_sibling(i).start()

    for t in range(2):
        for ok, up in ((r["upper"], True), (r["lower"], False)):
            @pl.when(ok)
            def _(t=t, up=up):
                to_halo(t, up).start()

    for i in range(CHUNKS):
        t, rows = i // (CHUNKS // 2), pl.ds((i % (CHUNKS // 2)) * ROWS, ROWS)
        to_sibling(i).wait_recv()
        total[t, rows] = sinks[core, t, rows].astype(jnp.float32) + sib_in[i].astype(jnp.float32)

        @pl.when(r["up"])
        def _(i=i, t=t, rows=rows):
            to_down(i).wait_recv()
            total[t, rows] += tree_in[i].astype(jnp.float32)

        @pl.when(r["root"])
        def _(i=i, t=t, rows=rows):
            to_side(i).wait_recv()
            total[t, rows] += side_in[i].astype(jnp.float32)

        @pl.when(jnp.logical_not(r["root"]))
        def _(i=i, t=t, rows=rows):
            tree_out[i] = total[t, rows].astype(jnp.bfloat16)

        @pl.when(r["down"])
        def _(i=i):
            to_down(i).start()

        @pl.when(r["side"])
        def _(i=i):
            to_side(i).start()

    for i in range(CHUNKS):
        to_sibling(i).wait_send()

        @pl.when(r["down"])
        def _(i=i):
            to_down(i).wait_send()

        @pl.when(r["side"])
        def _(i=i):
            to_side(i).wait_send()

    for t in range(2):
        for ok, up in ((r["upper"], True), (r["lower"], False)):
            @pl.when(ok)
            def _(t=t, up=up):
                to_halo(t, up).wait_send()
        for ok, up in ((r["lower"], True), (r["upper"], False)):
            @pl.when(ok)
            def _(t=t, up=up):
                to_halo(t, up).wait_recv()


def gather(window, sinks, n):
    part = pltpu.VMEM((CHUNKS, ROWS, WIDTH), jnp.bfloat16)
    return pl.pallas_call(
        functools.partial(gather_kernel, n),
        out_shape=(
            jax.ShapeDtypeStruct((2, 2, BLK, WIDTH), jnp.bfloat16),
            jax.ShapeDtypeStruct((2, BLK, WIDTH), jnp.float32),
        ),
        in_specs=[ANY, VMEM],
        out_specs=(ANY, VMEM),
        scratch_shapes=[part] * 4 + [pltpu.SemaphoreType.DMA((CHUNKS,))] * 5
        + [pltpu.SemaphoreType.DMA((2, 2)), pltpu.SemaphoreType.DMA((2, 2))],
        compiler_params=pltpu.CompilerParams(
            collective_id=1, has_side_effects=True, vmem_limit_bytes=48 << 20),
        cost_estimate=pl.CostEstimate(flops=40_000_000_000, bytes_accessed=8 << 20, transcendentals=0),
        name="gather_terms",
    )(window, sinks)


def pick_kernel(count, most, wanted, keys, values, outbox, sem):
    def body(i, _):
        h = jnp.maximum(wanted[i], 0)
        cols = pl.ds(pl.multiple_of(h * HD, HD), HD)
        d, k = i // most, lax.rem(i, most)
        pltpu.make_async_copy(keys.at[:, cols], outbox.at[d, k, 0], sem).start()
        pltpu.make_async_copy(values.at[:, cols], outbox.at[d, k, 1], sem).start()
        return 0

    lax.fori_loop(0, count, body, 0)
    pltpu.make_async_copy(outbox, outbox, sem).wait()


def pick(wanted, keys, values, n, most):
    return pl.pallas_call(
        functools.partial(pick_kernel, n * most, most),
        out_shape=jax.ShapeDtypeStruct((n, most, 2, BLK, HD), jnp.bfloat16),
        in_specs=[SMEM, ANY, ANY],
        out_specs=ANY,
        scratch_shapes=[pltpu.SemaphoreType.DMA],
        cost_estimate=pl.CostEstimate(flops=0, bytes_accessed=6 << 20, transcendentals=0),
        name="pick",
    )(wanted.reshape(-1), keys, values)


def dot(a, b, da, db):
    return lax.dot_general(a, b, (((da,), (db,)), ((), ())), preferred_element_type=jnp.float32)


def core_kernel(n, where, q_ref, g_ref, k_ref, v_ref, near, far0, far1, far2,
                gq_ref, own_ref, window_ref, sink_ref, outbox, terms, sem):
    h = pl.program_id(0)
    slot = lax.rem(h, 2)
    me = where[6 * H]
    lower, upper = me > 0, me < n - 1
    q, g = q_ref[...], g_ref[...]
    zero = jnp.zeros((BLK, HD), jnp.bfloat16)

    def sends(s, hh):
        return [
            pltpu.make_async_copy(
                terms.at[s, j], outbox.at[where[3 * hh + j], where[3 * H + 3 * hh + j]], sem.at[s, j])
            for j in range(3)
        ]

    ks, vs = [], []
    for t, out in ((0, ks), (1, vs)):
        out.append(jnp.where(lower, near[0, t], zero))
        out.append((k_ref, v_ref)[t][...])
        out.append(jnp.where(upper, near[1, t], zero))
        out.append(near[2, t])
        out.append(near[3, t])
        out += [f[0, 0, t] for f in (far0, far1, far2)]
    kc = jnp.concatenate(ks, axis=0)
    vc = jnp.concatenate(vs, axis=0)
    s = dot(kc, q, 1, 1) * SCALE
    row = lax.broadcasted_iota(jnp.int32, (8 * BLK, BLK), 0)
    first = jnp.where(lower, 0, BLK)
    skip = jnp.where(upper, 8 * BLK, 2 * BLK)
    ok = (row >= first) & ((row < skip) | (row >= 3 * BLK))
    s = jnp.where(ok, s, -jnp.inf)
    m = jnp.max(s, axis=0, keepdims=True)
    e = jnp.exp(s - m)
    p = e * (1.0 / jnp.sum(e, axis=0, keepdims=True))
    pb = p.astype(jnp.bfloat16)
    dp = dot(vc, g, 1, 1)
    delta = jnp.sum(pb.astype(jnp.float32) * dp, axis=0, keepdims=True)
    ds = (p * (dp - delta)).astype(jnp.bfloat16)
    gq_ref[...] = (dot(ds, kc, 0, 0) * SCALE).astype(jnp.bfloat16)
    kt = dot(ds, q, 1, 0) * SCALE
    vt = dot(pb, g, 1, 0)

    @pl.when(h >= 2)
    def _():
        for c in sends(slot, h - 2):
            c.wait()

    for t, term in ((0, kt), (1, vt)):
        def at(j, term=term):
            return term[j * BLK:(j + 1) * BLK]

        window_ref[0, t] = at(0).astype(jnp.bfloat16)
        own_ref[0, t] = at(1)
        window_ref[1, t] = at(2).astype(jnp.bfloat16)
        sink_ref[0, t] = at(3).astype(jnp.bfloat16)
        sink_ref[1, t] = at(4).astype(jnp.bfloat16)
        for j in range(3):
            terms[slot, j, t] = at(5 + j).astype(jnp.bfloat16)
    for c in sends(slot, h):
        c.start()

    @pl.when(h == H - 1)
    def _():
        for c in sends(1 - slot, h - 1) + sends(slot, h):
            c.wait()


def attend(where, q, g, k, v, near, fetched, n, most):
    col = pl.BlockSpec((BLK, HD), lambda h, w: (0, h))

    def far(j):
        return pl.BlockSpec(
            (1, 1, 2, BLK, HD), lambda h, w: (w[3 * h + j], w[3 * H + 3 * h + j], 0, 0, 0))

    return pl.pallas_call(
        functools.partial(core_kernel, n),
        out_shape=(
            jax.ShapeDtypeStruct((BLK, WIDTH), jnp.bfloat16),
            jax.ShapeDtypeStruct((H, 2, BLK, HD), jnp.float32),
            jax.ShapeDtypeStruct((2, 2, BLK, WIDTH), jnp.bfloat16),
            jax.ShapeDtypeStruct((2, 2, BLK, WIDTH), jnp.bfloat16),
            jax.ShapeDtypeStruct((n, most, 2, BLK, HD), jnp.bfloat16),
        ),
        grid_spec=pltpu.PrefetchScalarGridSpec(
            num_scalar_prefetch=1,
            grid=(H,),
            in_specs=[col, col, col, col,
                      pl.BlockSpec((4, 2, BLK, HD), lambda h, w: (0, 0, 0, h)),
                      far(0), far(1), far(2)],
            out_specs=(
                col,
                pl.BlockSpec((1, 2, BLK, HD), lambda h, w: (h, 0, 0, 0)),
                pl.BlockSpec((2, 2, BLK, HD), lambda h, w: (0, 0, 0, h)),
                pl.BlockSpec((2, 2, BLK, HD), lambda h, w: (0, 0, 0, h)),
                ANY,
            ),
            scratch_shapes=[
                pltpu.VMEM((2, 3, 2, BLK, HD), jnp.bfloat16),
                pltpu.SemaphoreType.DMA((2, 3)),
            ],
        ),
        compiler_params=pltpu.CompilerParams(vmem_limit_bytes=48 << 20),
        cost_estimate=pl.CostEstimate(flops=3_000_000_000, bytes_accessed=24 << 20, transcendentals=2 << 20),
        name="attend",
    )(where, q, g, k, v, near, fetched, fetched, fetched)


def combine_kernel(n, most, wanted, own, halo, sinks, returned, gk_ref, gv_ref, acc):
    me = wanted[n * most]
    lower, upper, root = me > 0, me < n - 1, me < 2
    for h in range(H):
        cols = slice(h * HD, (h + 1) * HD)
        for t in range(2):
            acc[h, t] = (
                own[h, t]
                + jnp.where(lower, halo[0, t, :, cols].astype(jnp.float32), 0.0)
                + jnp.where(upper, halo[1, t, :, cols].astype(jnp.float32), 0.0)
                + jnp.where(root, sinks[t, :, cols], 0.0)
            )

    def body(i, _):
        h = wanted[i]

        @pl.when(h >= 0)
        def _():
            acc[h] += returned[i].astype(jnp.float32)

        return 0

    lax.fori_loop(0, n * most, body, 0)
    for h in range(H):
        cols = slice(h * HD, (h + 1) * HD)
        gk_ref[:, cols] = acc[h, 0].astype(jnp.bfloat16)
        gv_ref[:, cols] = acc[h, 1].astype(jnp.bfloat16)


def combine(wanted, own, halo, sinks, returned, n, most):
    out = jax.ShapeDtypeStruct((BLK, WIDTH), jnp.bfloat16)
    return pl.pallas_call(
        functools.partial(combine_kernel, n, most),
        out_shape=(out, out),
        in_specs=[SMEM, VMEM, VMEM, VMEM, VMEM],
        out_specs=(VMEM, VMEM),
        scratch_shapes=[pltpu.VMEM((H, 2, BLK, HD), jnp.float32)],
        compiler_params=pltpu.CompilerParams(vmem_limit_bytes=48 << 20),
        cost_estimate=pl.CostEstimate(flops=4_000_000, bytes_accessed=9 << 20, transcendentals=0),
        name="combine",
    )(wanted, own, halo, sinks, returned.reshape(n * most, 2, BLK, HD))


def per_device(queries, keys, values, grad_out, partners):
    n = lax.axis_size("seq")
    me = lax.axis_index("seq").astype(jnp.int32)
    most = max(2, (3 * H + n - 1) // n)
    items = 3 * H
    dests = partners.reshape(items)
    heads = jnp.arange(items, dtype=jnp.int32) // 3
    order = jnp.arange(items)
    same = (dests[:, None] == dests[None, :]) & (order[None, :] < order[:, None])
    rank = jnp.sum(same.astype(jnp.int32), axis=1)
    places = jnp.arange(n * most, dtype=jnp.int32)
    hit = places[:, None] == (dests * most + rank)[None, :]
    requests = jnp.max(jnp.where(hit, heads[None, :], -1), axis=1).reshape(n, most)
    wanted = lax.all_to_all(requests, "seq", split_axis=0, concat_axis=0, tiled=True).reshape(-1)
    picked = pick(wanted, keys, values, n, most)
    fetched = lax.all_to_all(picked, "seq", split_axis=0, concat_axis=0, tiled=True)
    near = spread(keys, values, n)
    where = jnp.concatenate([dests, rank, me[None]])
    grad_queries, own, window, sinks, outbox = attend(
        where, queries, grad_out, keys, values, near, fetched, n, most)
    returned = lax.all_to_all(outbox, "seq", split_axis=0, concat_axis=0, tiled=True)
    halo, total = gather(window, sinks, n)
    table = jnp.concatenate([wanted, me[None]])
    grad_keys, grad_values = combine(table, own, halo, total, returned, n, most)
    return grad_queries, grad_keys, grad_values


def solution(mesh):
    block = P(("groups", "seq"), None)
    return jax.shard_map(
        per_device,
        mesh=mesh,
        in_specs=(block, block, block, block, P(("groups", "seq"), None, None)),
        out_specs=(block, block, block),
        check_vma=False,
    )
```

time: 460 us -> 379 us (0.82)
  Pallas kernels: 0 us -> 309 us
  waiting for transfers between devices: 291 us -> 0.01 us
  local copies, waits for them, and re-layouts: 77 us -> 10.4 us
  matrix products: 31.2 us -> 0 us
  other arithmetic: 20.4 us -> 1.13 us
  starting transfers between devices: 25.4 us -> 44 us
  between operations: 14.5 us -> 0.76 us
  blocking collectives: 0 us -> 13.6 us
    pallas_call x0 -> x5, Pallas kernels: none -> 309 us  [the longest x1 109 us: gather(): pl.pallas_call(functools.partial(gather_kernel, n), out_shape=(jax.ShapeD...]
    psum x2 -> x0, waiting for transfers between devices: 271 us -> none  [the longest x1 169 us: broadcast(): return lax.psum(block, axis)]
    all_to_all x1, starting transfers between devices: 4.48 us -> 39.3 us  [per_device(): lax.all_to_all(outbox, 'seq', split_axis=0, concat_axis=0, tiled=True)]
    dot_general x13 -> x0, matrix products: 31.2 us -> none  [the longest x1 5.7 us: per_device(): jnp.einsum('thd,khd->htk', grad_heads, near_values, preferred_element_typ...]
    all_to_all x1, waiting for transfers between devices: 14.6 us -> 0.01 us  [per_device(): lax.all_to_all(outbox, 'seq', split_axis=0, concat_axis=0, tiled=True)]
    all_to_all x0 -> x1, blocking collectives: none -> 13.6 us  [per_device(): lax.all_to_all(requests, 'seq', split_axis=0, concat_axis=0, tiled=True)]
    unnamed x43 -> x19, local copies, waits for them, and re-layouts: 22.3 us -> 9.08 us
    another operation x6 -> x0, other arithmetic: 12.6 us -> none
  transfers between devices with their start and end apart: 9 -> 2, of which waited for: 5 -> 0; matrix products, arithmetic and copies ran while one was open for 16% -> 0% of each run, Pallas kernels for 0% -> 49%
where the time goes in v1:
time: 379 us
  Pallas kernels  309 us (82%)
  starting transfers between devices  44 us (12%)
  blocking collectives  13.6 us (4%)
  local copies, waits for them, and re-layouts  10.4 us (3%)
    pallas_call x1, Pallas kernels, gather(): pl.pallas_call(functools.partial(gather_kernel, n), out_shape=(jax.ShapeD...  109 us
    pallas_call x1, Pallas kernels, pick(): pl.pallas_call(functools.partial(pick_kernel, n * most, most), out_shape=...  97.1 us
    pallas_call x1, Pallas kernels, spread(): pl.pallas_call(functools.partial(spread_kernel, n), out_shape=jax.ShapeDt...  74.6 us
    all_to_all x1, starting transfers between devices, per_device(): lax.all_to_all(outbox, 'seq', split_axis=0, concat_axis=0, tiled=True)  39.3 us
    pallas_call x1, Pallas kernels, attend(): pl.pallas_call(functools.partial(core_kernel, n), out_shape=(jax.ShapeDty...  22.7 us
    all_to_all x1, blocking collectives, per_device(): lax.all_to_all(requests, 'seq', split_axis=0, concat_axis=0, tiled=True)  13.6 us
    unnamed x19, local copies, waits for them, and re-layouts  9.08 us
  transfers between devices with their start and end apart: 2, of which 0 were waited for; matrix products, arithmetic and copies ran while one was open for 0% of the time, Pallas kernels for 49%

profile of v1, /device:TPU:0, one launch (start us, length us, event | category | flops | bytes accessed | tf_op | source)
XLA Modules:
  0.0 378.9 jit_solution(2696962842669766424)
XLA Ops:
  0.6 0.8 copy.12
  1.4 0.1 reshape.43
  1.5 0.2 convert_reduce_fusion
  1.7 0.1 select_reduce_fusion
  1.8 0.1 all_to_all.12
  1.9 13.6 %all_to_all.19 = s32[16,1,3]{2,1,0:T(1,128)S(1)} all-to-all(s32[16,1,3]{2,1,0:T(1,128)S(1)} %bitcast.3), channel_id=1, replica_groups=mesh['groups'=2,'seq'=16] {'seq'}, dimensions={0} | all-to-all | bytes 384 | tf_op jit(solution)/shard_map/all_to_all | solution.py:447
  15.5 0.5 broadcast.28
  16.0 0.7 reduce.3
  16.7 0.6 reshape.44.wanted
  17.3 97.1 %pick.1 = bf16[16,3,2,128,128]{4,3,2,1,0:T(8,128)(2,1)} custom-call(s32[48]{0:T(128)} %reshape.44.wanted, bf16[128,2048]{1,0:T(8,128)(2,1)} %k_ref.1, bf16[128,2048]{1,0:T(8,128)(2,1)} %v_ref.1), custom_call_target="tpu_custom_call" | custom-call | bytes 6291456 | tf_op jit(solution)/shard_map/pick/pallas_call | solution.py:268
  114.3 0.0 copy-start.4
  114.4 0.0 copy-start.5
  114.4 4.6 %all-to-all-start.1 = ((bf16[16,3,2,128,128]{4,3,2,1,0:T(8,128)(2,1)}), bf16[16,3,2,128,128]{4,3,2,1,0:T(8,128)(2,1)}, u32[]{:S(2)}, u32[]{:S(2)}) async-start(bf16[16,3,2,128,128]{4,3,2,1,0:T(8,128)(2,1)} %pick.1), calls=%async_computation.1 | async-start | bytes 6291456 | tf_op jit(solution)/shard_map/all_to_all | solution.py:449
  119.0 0.1 pad_add_fusion.where
  119.1 0.0 copy-done.4
  119.1 0.0 copy-done.5
  119.1 74.6 %spread.1.near = bf16[4,2,128,2048]{3,2,1,0:T(8,128)(2,1)S(1)} custom-call(bf16[128,2048]{1,0:T(8,128)(2,1)S(1)} %copy-done.4, bf16[128,2048]{1,0:T(8,128)(2,1)S(1)} %copy-done.5), custom_call_target="tpu_custom_call" | custom-call | flops 40000000000 | bytes 8388608 | tf_op jit(solution)/shard_map/spread/pallas_call | solution.py:144
  193.7 0.0 copy-start
  193.7 1.9 copy-done
  195.6 0.0 all-to-all-done.1.far0.far1.far2
  195.6 0.0 copy-start.6
  195.6 1.0 copy-done.6
  196.7 0.0 copy-start.7
  196.7 1.0 copy-done.7
  197.7 22.7 %attend.1 = (bf16[128,2048]{1,0:T(8,128)(2,1)}, f32[16,2,128,128]{3,2,1,0:T(8,128)S(1)}, bf16[2,2,128,2048]{3,2,1,0:T(8,128)(2,1)}, bf16[2,2,128,2048]{3,2,1,0:T(8,128)(2,1)}, bf16[16,3,2,128,128]{4,3,2,1,0:T(8,128)(2,1)}) custom-call(s32[97]{0:T(128)S(1)} %pad_add_fusion.where, bf16[128,2048]{1,0:T(8,128)(2,1)S(1)} %copy-done.6, ...), custom_call_target="tpu_custom_call" | custom-call | flops 3000000000 | bytes 25165824 | tf_op jit(solution)/shard_map/attend/pallas_call | solution.py:358
  220.4 0.0 copy-start.8
  220.5 39.3 %all-to-all-start.2 = ((bf16[16,3,2,128,128]{4,3,2,1,0:T(8,128)(2,1)}), bf16[16,3,2,128,128]{4,3,2,1,0:T(8,128)(2,1)}, u32[]{:S(2)}, u32[]{:S(2)}) async-start(bf16[16,3,2,128,128]{4,3,2,1,0:T(8,128)(2,1)} %get-tuple-element.18), calls=%async_computation.2 | async-start | bytes 6291456 | tf_op jit(solution)/shard_map/all_to_all | solution.py:454
  259.8 0.0 copy-done.8
  259.8 0.1 pad_add_fusion.1.wanted
  259.9 109.3 %gather_terms.1 = (bf16[2,2,128,2048]{3,2,1,0:T(8,128)(2,1)S(1)}, f32[2,128,2048]{2,1,0:T(8,128)S(1)}) custom-call(bf16[2,2,128,2048]{3,2,1,0:T(8,128)(2,1)} %get-tuple-element.14.window, bf16[2,2,128,2048]{3,2,1,0:T(8,128)(2,1)} %get-tuple-element.15.sinks), custom_call_target="tpu_custom_call" | custom-call | flops 40000000000 | bytes 8388608 | tf_op jit(solution)/shard_map/gather_terms/pallas_call | solution.py:237
  369.2 0.0 copy-start.1
  369.2 1.3 copy-done.1
  370.5 0.0 copy-start.3
  370.5 1.4 copy-done.3
  371.9 0.0 all-to-all-done.2
  371.9 0.0 copy-start.2
  371.9 1.6 copy-done.2
  373.5 5.4 %combine.1 = (bf16[128,2048]{1,0:T(8,128)(2,1)}, bf16[128,2048]{1,0:T(8,128)(2,1)}) custom-call(s32[49]{0:T(128)S(1)} %pad_add_fusion.1.wanted, f32[16,2,128,128]{3,2,1,0:T(8,128)S(1)} %get-tuple-element.13.own, bf16[2,2,128,2048]{3,2,1,0:T(8,128)(2,1)S(1)} %copy-done.2, f32[2,128,2048]{2,1,0:T(8,128)} %copy-done.3, bf16[48,2,128,128]{3,2,1,0:T(8,128)(2,1)} %bitcast.2.returned), custom_call_target="tpu_custom_call" | custom-call | flops 4000000 | bytes 9437184 | tf_op jit(solution)/shard_map/combine/pallas_call | solution.py:422
  (1 shorter events, 0.0 us)
Async XLA Ops:
  114.3 4.8 %copy-start.4 = (bf16[128,2048]{1,0:T(8,128)(2,1)S(1)}, bf16[128,2048]{1,0:T(8,128)(2,1)}, u32[]{:S(2)}) copy-start(bf16[128,2048]{1,0:T(8,128)(2,1)} %k_ref.1) | copy-start | bytes 1572868
  114.4 4.7 %copy-start.5 = (bf16[128,2048]{1,0:T(8,128)(2,1)S(1)}, bf16[128,2048]{1,0:T(8,128)(2,1)}, u32[]{:S(2)}) copy-start(bf16[128,2048]{1,0:T(8,128)(2,1)} %v_ref.1) | copy-start | bytes 1572868
  114.4 81.2 %all-to-all-start.1 = ((bf16[16,3,2,128,128]{4,3,2,1,0:T(8,128)(2,1)}), bf16[16,3,2,128,128]{4,3,2,1,0:T(8,128)(2,1)}, u32[]{:S(2)}, u32[]{:S(2)}) async-start(bf16[16,3,2,128,128]{4,3,2,1,0:T(8,128)(2,1)} %pick.1), calls=%async_computation.1 | async-start | bytes 6291456 | tf_op jit(solution)/shard_map/all_to_all | solution.py:449
  193.7 1.9 copy-start
  195.6 1.0 copy-start.6
  196.7 1.0 copy-start.7
  220.4 39.3 %copy-start.8 = (s32[48]{0:T(128)S(1)}, s32[48]{0:T(128)}, u32[]{:S(2)}) copy-start(s32[48]{0:T(128)} %reshape.44.wanted) | copy-start | bytes 580
  220.5 151.5 %all-to-all-start.2 = ((bf16[16,3,2,128,128]{4,3,2,1,0:T(8,128)(2,1)}), bf16[16,3,2,128,128]{4,3,2,1,0:T(8,128)(2,1)}, u32[]{:S(2)}, u32[]{:S(2)}) async-start(bf16[16,3,2,128,128]{4,3,2,1,0:T(8,128)(2,1)} %get-tuple-element.18), calls=%async_computation.2 | async-start | bytes 6291456 | tf_op jit(solution)/shard_map/all_to_all | solution.py:454
  369.2 1.3 copy-start.1
  370.5 1.4 copy-start.3
  371.9 1.6 copy-start.2

commit v2 on v1

--- a/solution.py
+++ b/solution.py
@@ -251,13 +251,20 @@
     )(window, sinks)
 
 
-def pick_kernel(count, most, wanted, keys, values, outbox, sem):
+def pick_kernel(count, most, wanted, keys, values, outbox, held, sem_in, sem):
+    loads = []
+    for h in range(H):
+        cols = pl.ds(h * HD, HD)
+        loads.append(pltpu.make_async_copy(keys.at[:, cols], held.at[h, 0], sem_in.at[h, 0]))
+        loads.append(pltpu.make_async_copy(values.at[:, cols], held.at[h, 1], sem_in.at[h, 1]))
+    for c in loads:
+        c.start()
+    for c in loads:
+        c.wait()
+
     def body(i, _):
         h = jnp.maximum(wanted[i], 0)
-        cols = pl.ds(pl.multiple_of(h * HD, HD), HD)
-        d, k = i // most, lax.rem(i, most)
-        pltpu.make_async_copy(keys.at[:, cols], outbox.at[d, k, 0], sem).start()
-        pltpu.make_async_copy(values.at[:, cols], outbox.at[d, k, 1], sem).start()
+        pltpu.make_async_copy(held.at[h], outbox.at[i // most, lax.rem(i, most)], sem).start()
         return 0
 
     lax.fori_loop(0, count, body, 0)
@@ -270,8 +277,10 @@
         out_shape=jax.ShapeDtypeStruct((n, most, 2, BLK, HD), jnp.bfloat16),
         in_specs=[SMEM, ANY, ANY],
         out_specs=ANY,
-        scratch_shapes=[pltpu.SemaphoreType.DMA],
+        scratch_shapes=[pltpu.VMEM((H, 2, BLK, HD), jnp.bfloat16),
+                        pltpu.SemaphoreType.DMA((H, 2)), pltpu.SemaphoreType.DMA],
         cost_estimate=pl.CostEstimate(flops=0, bytes_accessed=6 << 20, transcendentals=0),
+        compiler_params=pltpu.CompilerParams(vmem_limit_bytes=48 << 20),
         name="pick",
     )(wanted.reshape(-1), keys, values)
 

time: 379 us -> 287 us (0.76)
  Pallas kernels: 309 us -> 215 us
    pallas_call x1, Pallas kernels: 97.1 us -> 2.84 us  [pick(): pl.pallas_call(functools.partial(pick_kernel, n * most, most), out_shape=...]
    unnamed x19 -> x21, local copies, waits for them, and re-layouts: 9.08 us -> 11.2 us
  transfers between devices with their start and end apart: 2 -> 2, of which waited for: 0 -> 0; matrix products, arithmetic and copies ran while one was open for 0% -> 0% of each run, Pallas kernels for 49% -> 64%
where the time goes in v2:
time: 287 us; the launch traced here: 286 us
  Pallas kernels  215 us (75%)
  starting transfers between devices  44 us (15%)
  blocking collectives  13.6 us (5%)
  local copies, waits for them, and re-layouts  11.9 us (4%)
    pallas_call x1, Pallas kernels, gather(): pl.pallas_call(functools.partial(gather_kernel, n), out_shape=(jax.ShapeD...  109 us
    pallas_call x1, Pallas kernels, spread(): pl.pallas_call(functools.partial(spread_kernel, n), out_shape=jax.ShapeDt...  74.6 us
    all_to_all x1, starting transfers between devices, per_device(): lax.all_to_all(outbox, 'seq', split_axis=0, concat_axis=0, tiled=True)  39.3 us
    pallas_call x1, Pallas kernels, attend(): pl.pallas_call(functools.partial(core_kernel, n), out_shape=(jax.ShapeDty...  22.7 us
    all_to_all x1, blocking collectives, per_device(): lax.all_to_all(requests, 'seq', split_axis=0, concat_axis=0, tiled=True)  13.6 us
    unnamed x21, local copies, waits for them, and re-layouts  11.2 us
  transfers between devices with their start and end apart: 2, of which 0 were waited for; matrix products, arithmetic and copies ran while one was open for 0% of the time, Pallas kernels for 64%

profile of v2, /device:TPU:0, one launch (start us, length us, event | category | flops | bytes accessed | tf_op | source)
XLA Modules:
  0.0 286.3 jit_solution(8582580949020858298)
XLA Ops:
  0.6 0.8 copy.12
  1.4 0.1 reshape.43
  1.5 0.2 convert_reduce_fusion
  1.7 0.1 select_reduce_fusion
  1.8 0.1 all_to_all.12
  1.9 13.6 %all_to_all.19 = s32[16,1,3]{2,1,0:T(1,128)S(1)} all-to-all(s32[16,1,3]{2,1,0:T(1,128)S(1)} %bitcast.3), channel_id=1, replica_groups=mesh['groups'=2,'seq'=16] {'seq'}, dimensions={0} | all-to-all | bytes 384 | tf_op jit(solution)/shard_map/all_to_all | solution.py:456
  15.5 0.5 broadcast.28
  16.0 0.7 reduce.3
  16.7 0.1 reshape.44.wanted
  16.8 0.0 copy-start.4
  16.8 1.0 copy-done.4
  17.8 0.0 copy-start.6
  17.8 1.0 copy-done.6
  18.8 2.8 pick.1
  21.7 0.0 copy-start.5
  21.7 0.0 copy-start.7
  21.7 4.6 %all-to-all-start.1 = ((bf16[16,3,2,128,128]{4,3,2,1,0:T(8,128)(2,1)}), bf16[16,3,2,128,128]{4,3,2,1,0:T(8,128)(2,1)}, u32[]{:S(2)}, u32[]{:S(2)}) async-start(bf16[16,3,2,128,128]{4,3,2,1,0:T(8,128)(2,1)} %pick.1), calls=%async_computation.1 | async-start | bytes 6291456 | tf_op jit(solution)/shard_map/all_to_all | solution.py:458
  26.3 0.1 pad_add_fusion.where
  26.4 0.0 copy-done.5
  26.4 0.0 copy-done.7
  26.4 74.6 %spread.1.near = bf16[4,2,128,2048]{3,2,1,0:T(8,128)(2,1)S(1)} custom-call(bf16[128,2048]{1,0:T(8,128)(2,1)S(1)} %copy-done.5, bf16[128,2048]{1,0:T(8,128)(2,1)S(1)} %copy-done.7), custom_call_target="tpu_custom_call" | custom-call | flops 40000000000 | bytes 8388608 | tf_op jit(solution)/shard_map/spread/pallas_call | solution.py:144
  101.0 0.0 copy-start
  101.0 1.9 copy-done
  102.9 0.0 all-to-all-done.1.far0.far1.far2
  102.9 0.0 copy-start.8
  102.9 1.0 copy-done.8
  104.0 0.0 copy-start.9
  104.0 1.0 copy-done.9
  105.0 22.7 %attend.1 = (bf16[128,2048]{1,0:T(8,128)(2,1)}, f32[16,2,128,128]{3,2,1,0:T(8,128)S(1)}, bf16[2,2,128,2048]{3,2,1,0:T(8,128)(2,1)}, bf16[2,2,128,2048]{3,2,1,0:T(8,128)(2,1)}, bf16[16,3,2,128,128]{4,3,2,1,0:T(8,128)(2,1)}) custom-call(s32[97]{0:T(128)S(1)} %pad_add_fusion.where, bf16[128,2048]{1,0:T(8,128)(2,1)S(1)} %copy-done.8, ...), custom_call_target="tpu_custom_call" | custom-call | flops 3000000000 | bytes 25165824 | tf_op jit(solution)/shard_map/attend/pallas_call | solution.py:367
  127.7 39.3 %all-to-all-start.2 = ((bf16[16,3,2,128,128]{4,3,2,1,0:T(8,128)(2,1)}), bf16[16,3,2,128,128]{4,3,2,1,0:T(8,128)(2,1)}, u32[]{:S(2)}, u32[]{:S(2)}) async-start(bf16[16,3,2,128,128]{4,3,2,1,0:T(8,128)(2,1)} %get-tuple-element.18), calls=%async_computation.2 | async-start | bytes 6291456 | tf_op jit(solution)/shard_map/all_to_all | solution.py:463
  167.1 0.1 pad_add_fusion.1.wanted
  167.2 109.3 %gather_terms.1 = (bf16[2,2,128,2048]{3,2,1,0:T(8,128)(2,1)S(1)}, f32[2,128,2048]{2,1,0:T(8,128)S(1)}) custom-call(bf16[2,2,128,2048]{3,2,1,0:T(8,128)(2,1)} %get-tuple-element.14.window, bf16[2,2,128,2048]{3,2,1,0:T(8,128)(2,1)} %get-tuple-element.15.sinks), custom_call_target="tpu_custom_call" | custom-call | flops 40000000000 | bytes 8388608 | tf_op jit(solution)/shard_map/gather_terms/pallas_call | solution.py:237
  276.5 0.0 copy-start.1
  276.5 1.3 copy-done.1
  277.8 0.0 copy-start.3
  277.8 1.4 copy-done.3
  279.2 0.0 all-to-all-done.2
  279.2 0.0 copy-start.2
  279.2 1.6 copy-done.2
  280.8 5.5 %combine.1 = (bf16[128,2048]{1,0:T(8,128)(2,1)}, bf16[128,2048]{1,0:T(8,128)(2,1)}) custom-call(s32[49]{0:T(128)S(1)} %pad_add_fusion.1.wanted, f32[16,2,128,128]{3,2,1,0:T(8,128)S(1)} %get-tuple-element.13.own, bf16[2,2,128,2048]{3,2,1,0:T(8,128)(2,1)S(1)} %copy-done.2, f32[2,128,2048]{2,1,0:T(8,128)} %copy-done.3, bf16[48,2,128,128]{3,2,1,0:T(8,128)(2,1)} %bitcast.2.returned), custom_call_target="tpu_custom_call" | custom-call | flops 4000000 | bytes 9437184 | tf_op jit(solution)/shard_map/combine/pallas_call | solution.py:431
  (1 shorter events, 0.0 us)
Async XLA Ops:
  16.8 1.0 copy-start.4
  17.8 1.0 copy-start.6
  21.7 4.7 %copy-start.5 = (bf16[128,2048]{1,0:T(8,128)(2,1)S(1)}, bf16[128,2048]{1,0:T(8,128)(2,1)}, u32[]{:S(2)}) copy-start(bf16[128,2048]{1,0:T(8,128)(2,1)} %k_ref.1) | copy-start | bytes 1572868
  21.7 4.7 %copy-start.7 = (bf16[128,2048]{1,0:T(8,128)(2,1)S(1)}, bf16[128,2048]{1,0:T(8,128)(2,1)}, u32[]{:S(2)}) copy-start(bf16[128,2048]{1,0:T(8,128)(2,1)} %v_ref.1) | copy-start | bytes 1572868
  21.7 81.2 %all-to-all-start.1 = ((bf16[16,3,2,128,128]{4,3,2,1,0:T(8,128)(2,1)}), bf16[16,3,2,128,128]{4,3,2,1,0:T(8,128)(2,1)}, u32[]{:S(2)}, u32[]{:S(2)}) async-start(bf16[16,3,2,128,128]{4,3,2,1,0:T(8,128)(2,1)} %pick.1), calls=%async_computation.1 | async-start | bytes 6291456 | tf_op jit(solution)/shard_map/all_to_all | solution.py:458
  101.0 1.9 copy-start
  102.9 1.0 copy-start.8
  104.0 1.0 copy-start.9
  127.7 151.5 %all-to-all-start.2 = ((bf16[16,3,2,128,128]{4,3,2,1,0:T(8,128)(2,1)}), bf16[16,3,2,128,128]{4,3,2,1,0:T(8,128)(2,1)}, u32[]{:S(2)}, u32[]{:S(2)}) async-start(bf16[16,3,2,128,128]{4,3,2,1,0:T(8,128)(2,1)} %get-tuple-element.18), calls=%async_computation.2 | async-start | bytes 6291456 | tf_op jit(solution)/shard_map/all_to_all | solution.py:463
  276.5 1.3 copy-start.1
  277.8 1.4 copy-start.3
  279.2 1.6 copy-start.2

commit v3 on v1

v3 whole, which is shorter than its diff:
```python
import functools
import math

import jax
import jax.numpy as jnp
from jax import lax
from jax.experimental import pallas as pl
from jax.experimental.pallas import tpu as pltpu
from jax.sharding import PartitionSpec as P

H = 16
HD = 128
BLK = 128
WIDTH = H * HD
SCALE = 1.0 / math.sqrt(HD)
STRIDE = 4
CHUNKS = 4
WINDOW = 3
ROWS = 2 * BLK // CHUNKS
ANY = pl.BlockSpec(memory_space=pl.ANY)
VMEM = pl.BlockSpec(memory_space=pltpu.VMEM)
SMEM = pl.BlockSpec(memory_space=pltpu.SMEM)


def remote(src, dst, send, recv, target):
    return pltpu.make_async_remote_copy(
        src_ref=src, dst_ref=dst, send_sem=send, recv_sem=recv,
        device_id={"seq": target}, device_id_type=pl.DeviceIdType.MESH,
    )


def signs(n):
    me = lax.axis_index("seq")
    rung = me // STRIDE
    root, side = me < 2, jnp.logical_and(me >= 2, me < STRIDE)
    return dict(
        me=me,
        core=lax.rem(me, 2),
        sibling=me + 1 - 2 * lax.rem(me, 2),
        lower=me > 0,
        upper=me < n - 1,
        odd=lax.rem(me, 2) == 1,
        even=lax.rem(me, 2) == 0,
        root=root,
        side=side,
        down=me >= STRIDE,
        up=me + STRIDE < n,
        depth=rung + lax.rem(me, STRIDE) // 2,
        height=n // STRIDE - 1 - rung + root.astype(jnp.int32),
    )


def greet(n):
    me = lax.axis_index("seq")
    barrier = pltpu.get_barrier_semaphore()

    def hail(k, _):
        pl.semaphore_signal(barrier, inc=1, device_id={"seq": lax.rem(me + k, n)},
                            device_id_type=pl.DeviceIdType.MESH)
        return 0

    lax.fori_loop(1, n, hail, 0)
    pl.semaphore_wait(barrier, n - 1)


def offsets(n):
    wide = sorted(range(1, n), key=lambda k: (abs(k - n // 2), k))
    out = []
    while wide:
        out.append(wide.pop(0))
        if wide:
            out.append(wide.pop())
    return out


def piece(ref, lead, i):
    half = CHUNKS // 2
    return ref.at[lead, i // half, pl.ds(pl.multiple_of(lax.rem(i, half) * ROWS, ROWS), ROWS)]


def halo_starts(r, step, to_halo):
    early = ((r["even"], True), (r["odd"], False))
    late = ((jnp.logical_and(r["odd"], r["upper"]), True), (jnp.logical_and(r["even"], r["lower"]), False))
    for t in range(2):
        for sides, at in ((early, 0), (late, (3, 8)[t])):
            if step != at:
                continue
            for ok, up in sides:
                @pl.when(ok)
                def _(t=t, up=up):
                    to_halo(t, up).start()


def halo_waits(r, to_halo):
    for t in range(2):
        for ok, up in ((r["upper"], True), (r["lower"], False)):
            @pl.when(ok)
            def _(t=t, up=up):
                to_halo(t, up).wait_send()
        for ok, up in ((r["lower"], True), (r["upper"], False)):
            @pl.when(ok)
            def _(t=t, up=up):
                to_halo(t, up).wait_recv()


def fetch_kernel(n, most, asks, keys, values, near, fetched, wanted, held, ready, picks,
                 load, ask_s, ask_r, table, all_s, all_r, tree_s, tree_r, side_s, sib_s, sib_r,
                 halo_s, halo_r):
    r = signs(n)
    me, core, root = r["me"], r["core"], r["root"]
    loads = []
    for h in range(H):
        cols = pl.ds(h * HD, HD)
        loads.append(pltpu.make_async_copy(keys.at[:, cols], held.at[h, 0], load.at[h, 0]))
        loads.append(pltpu.make_async_copy(values.at[:, cols], held.at[h, 1], load.at[h, 1]))
    for c in loads:
        c.start()
    greet(n)

    def ask(k):
        peer = lax.rem(me + k, n)
        return remote(asks.at[peer], wanted.at[me], ask_s.at[peer], ask_r.at[me], peer)

    def asked(k):
        peer = lax.rem(me + k, n)
        return remote(asks.at[peer], wanted.at[peer], ask_s.at[peer], ask_r.at[peer], peer)

    for k in range(1, n):
        ask(k).start()
    mine = pltpu.make_async_copy(asks.at[me], wanted.at[me], table)
    mine.start()

    def own(t, i):
        return (keys, values)[t].at[pl.ds(pl.multiple_of(lax.rem(i, CHUNKS // 2) * ROWS, ROWS), ROWS)]

    def to_up(i, src):
        return remote(src, piece(near, 2 + core, i), tree_s.at[i], tree_r.at[i], me + STRIDE)

    def to_side(i, src):
        return remote(src, piece(near, 2 + core, i), side_s.at[i], tree_r.at[i], me + 2)

    def to_sibling(i, src):
        return remote(src, piece(near, 2 + core, i), sib_s.at[i], sib_r.at[i], r["sibling"])

    def from_sibling(i):
        return remote(piece(near, 3 - core, i), piece(near, 3 - core, i), sib_s.at[i], sib_r.at[i], r["sibling"])

    def keep(t):
        return pltpu.make_async_copy((keys, values)[t], near.at[2 + core, t], load.at[t, 0])

    def to_halo(t, up):
        slot = 0 if up else 1
        return remote((keys, values)[t], near.at[slot, t], halo_s.at[slot, t], halo_r.at[slot, t],
                      me + (1 if up else -1))

    def relay(i):
        for t in range(2):
            @pl.when(jnp.logical_and(root, i // (CHUNKS // 2) == t))
            def _(t=t):
                @pl.when(r["up"])
                def _():
                    to_up(i, own(t, i)).start()

                to_side(i, own(t, i)).start()
                to_sibling(i, own(t, i)).start()

        @pl.when(jnp.logical_not(root))
        def _():
            to_up(i, piece(near, 2 + core, i)).wait_recv()

            @pl.when(r["up"])
            def _():
                to_up(i, piece(near, 2 + core, i)).start()

            to_sibling(i, piece(near, 2 + core, i)).start()

    def relay_at(step):
        i = step - 2 * r["depth"]

        @pl.when(jnp.logical_and(i >= 0, i < CHUNKS))
        def _():
            relay(i)

    relay_at(0)
    halo_starts(r, 0, to_halo)
    for c in loads:
        c.wait()

    @pl.when(root)
    def _():
        for t in range(2):
            keep(t).start()

    for k in range(1, n):
        asked(k).wait_recv()
    mine.wait()
    copy = pltpu.make_async_copy(wanted, picks, table)
    copy.start()
    copy.wait()

    def fill(peer):
        for j in range(most):
            ready[peer, j] = held[jnp.maximum(picks[peer, 0, j], 0)]

    def send(k):
        peer = lax.rem(me + k, n)
        return remote(ready.at[peer], fetched.at[me], all_s.at[peer], all_r.at[me], peer)

    def sent(k):
        peer = lax.rem(me + k, n)
        return remote(ready.at[peer], fetched.at[peer], all_s.at[peer], all_r.at[peer], peer)

    hops = offsets(n)
    for step, k in enumerate(hops):
        fill(lax.rem(me + k, n))
        if step >= WINDOW:
            send(hops[step - WINDOW]).wait_send()
        send(k).start()
        if step:
            relay_at(step)
            halo_starts(r, step, to_halo)
    fill(me)
    self_copy = pltpu.make_async_copy(ready.at[me], fetched.at[me], table)
    self_copy.start()
    for k in hops[-WINDOW:]:
        send(k).wait_send()
    for k in hops:
        sent(k).wait_recv()
    for k in range(1, n):
        ask(k).wait_send()
    for i in range(CHUNKS):
        from_sibling(i).wait_recv()
        to_sibling(i, piece(near, 2 + core, i)).wait_send()

        @pl.when(r["up"])
        def _(i=i):
            to_up(i, piece(near, 2 + core, i)).wait_send()

        @pl.when(root)
        def _(i=i):
            to_side(i, piece(near, 2 + core, i)).wait_send()

    @pl.when(root)
    def _():
        for t in range(2):
            keep(t).wait()

    self_copy.wait()
    halo_waits(r, to_halo)


def fetch(asks, keys, values, n, most):
    dma = pltpu.SemaphoreType.DMA
    return pl.pallas_call(
        functools.partial(fetch_kernel, n, most),
        out_shape=(
            jax.ShapeDtypeStruct((4, 2, BLK, WIDTH), jnp.bfloat16),
            jax.ShapeDtypeStruct((n, most, 2, BLK, HD), jnp.bfloat16),
            jax.ShapeDtypeStruct((n, 1, 128), jnp.int32),
        ),
        in_specs=[VMEM, ANY, ANY],
        out_specs=(ANY, ANY, VMEM),
        scratch_shapes=[
            pltpu.VMEM((H, 2, BLK, HD), jnp.bfloat16),
            pltpu.VMEM((n, most, 2, BLK, HD), jnp.bfloat16),
            pltpu.SMEM((n, 1, 128), jnp.int32),
            dma((H, 2)), dma((n,)), dma((n,)), dma, dma((n,)), dma((n,)),
            dma((CHUNKS,)), dma((CHUNKS,)), dma((CHUNKS,)), dma((CHUNKS,)), dma((CHUNKS,)),
            dma((2, 2)), dma((2, 2)),
        ],
        compiler_params=pltpu.CompilerParams(
            collective_id=0, has_side_effects=True, vmem_limit_bytes=48 << 20),
        name="fetch",
    )(asks, keys, values)


def collect_kernel(n, outbox, window, sinks, returned, halo, total, sib_in, tree_in, side_in, tree_out,
                   table, all_s, all_r, tree_s, tree_r, side_r, sib_s, sib_r, halo_s, halo_r):
    r = signs(n)
    me, core = r["me"], r["core"]
    greet(n)

    def to_sibling(i):
        return remote(piece(sinks, 1 - core, i), sib_in.at[i], sib_s.at[i], sib_r.at[i], r["sibling"])

    def to_down(i):
        return remote(tree_out.at[i], tree_in.at[i], tree_s.at[i], tree_r.at[i], me - STRIDE)

    def to_side(i):
        return remote(tree_out.at[i], side_in.at[i], tree_s.at[i], side_r.at[i], me - 2)

    def to_halo(t, up):
        slot = 0 if up else 1
        return remote(window.at[1 - slot, t], halo.at[slot, t],
                      halo_s.at[slot, t], halo_r.at[slot, t], me + (1 if up else -1))

    def send(k):
        peer = lax.rem(me + k, n)
        return remote(outbox.at[peer], returned.at[me], all_s.at[peer], all_r.at[me], peer)

    def sent(k):
        peer = lax.rem(me + k, n)
        return remote(outbox.at[peer], returned.at[peer], all_s.at[peer], all_r.at[peer], peer)

    def add(i):
        half = CHUNKS // 2
        t, rows = i // half, pl.ds(pl.multiple_of(lax.rem(i, half) * ROWS, ROWS), ROWS)
        to_sibling(i).wait_recv()
        total[t, rows] = sinks[core, t, rows].astype(jnp.float32) + sib_in[i].astype(jnp.float32)

        @pl.when(r["up"])
        def _():
            to_down(i).wait_recv()
            total[t, rows] += tree_in[i].astype(jnp.float32)

        @pl.when(r["root"])
        def _():
            to_side(i).wait_recv()
            total[t, rows] += side_in[i].astype(jnp.float32)

        @pl.when(jnp.logical_not(r["root"]))
        def _():
            tree_out[i] = total[t, rows].astype(jnp.bfloat16)

        @pl.when(r["down"])
        def _():
            to_down(i).start()

        @pl.when(r["side"])
        def _():
            to_side(i).start()

    for i in range(CHUNKS):
        to_sibling(i).start()
    hops = offsets(n)
    for step, k in enumerate(hops):
        if step >= WINDOW:
            send(hops[step - WINDOW]).wait_send()
        send(k).start()
        halo_starts(r, step, to_halo)
        i = step - 2 * r["height"] - 1

        @pl.when(jnp.logical_and(i >= 0, i < CHUNKS))
        def _(i=i):
            add(i)

    self_copy = pltpu.make_async_copy(outbox.at[me], returned.at[me], table)
    self_copy.start()
    for k in hops[-WINDOW:]:
        send(k).wait_send()
    for k in hops:
        sent(k).wait_recv()
    for i in range(CHUNKS):
        to_sibling(i).wait_send()

        @pl.when(r["down"])
        def _(i=i):
            to_down(i).wait_send()

        @pl.when(r["side"])
        def _(i=i):
            to_side(i).wait_send()

    self_copy.wait()
    halo_waits(r, to_halo)


def collect(outbox, window, sinks, n, most):
    dma = pltpu.SemaphoreType.DMA
    part = pltpu.VMEM((CHUNKS, ROWS, WIDTH), jnp.bfloat16)
    return pl.pallas_call(
        functools.partial(collect_kernel, n),
        out_shape=(
            jax.ShapeDtypeStruct((n, most, 2, BLK, HD), jnp.bfloat16),
            jax.ShapeDtypeStruct((2, 2, BLK, WIDTH), jnp.bfloat16),
            jax.ShapeDtypeStruct((2, BLK, WIDTH), jnp.float32),
        ),
        in_specs=[ANY, ANY, VMEM],
        out_specs=(ANY, ANY, VMEM),
        scratch_shapes=[part] * 4 + [dma, dma((n,)), dma((n,))] + [dma((CHUNKS,))] * 5 + [dma((2, 2))] * 2,
        compiler_params=pltpu.CompilerParams(
            collective_id=1, has_side_effects=True, vmem_limit_bytes=48 << 20),
        name="collect",
    )(outbox, window, sinks)


def dot(a, b, da, db):
    return lax.dot_general(a, b, (((da,), (db,)), ((), ())), preferred_element_type=jnp.float32)


def core_kernel(n, where, q_ref, g_ref, k_ref, v_ref, near, far0, far1, far2,
                gq_ref, own_ref, window_ref, sink_ref, outbox, terms, sem):
    h = pl.program_id(0)
    slot = lax.rem(h, 2)
    me = where[6 * H]
    lower, upper = me > 0, me < n - 1
    q, g = q_ref[...], g_ref[...]
    zero = jnp.zeros((BLK, HD), jnp.bfloat16)

    def sends(s, hh):
        return [
            pltpu.make_async_copy(
                terms.at[s, j], outbox.at[where[3 * hh + j], where[3 * H + 3 * hh + j]], sem.at[s, j])
            for j in range(3)
        ]

    ks, vs = [], []
    for t, out in ((0, ks), (1, vs)):
        out.append(jnp.where(lower, near[0, t], zero))
        out.append((k_ref, v_ref)[t][...])
        out.append(jnp.where(upper, near[1, t], zero))
        out.append(near[2, t])
        out.append(near[3, t])
        out += [f[0, 0, t] for f in (far0, far1, far2)]
    kc = jnp.concatenate(ks, axis=0)
    vc = jnp.concatenate(vs, axis=0)
    s = dot(kc, q, 1, 1) * SCALE
    row = lax.broadcasted_iota(jnp.int32, (8 * BLK, BLK), 0)
    first = jnp.where(lower, 0, BLK)
    skip = jnp.where(upper, 8 * BLK, 2 * BLK)
    ok = (row >= first) & ((row < skip) | (row >= 3 * BLK))
    s = jnp.where(ok, s, -jnp.inf)
    m = jnp.max(s, axis=0, keepdims=True)
    e = jnp.exp(s - m)
    p = e * (1.0 / jnp.sum(e, axis=0, keepdims=True))
    pb = p.astype(jnp.bfloat16)
    dp = dot(vc, g, 1, 1)
    delta = jnp.sum(pb.astype(jnp.float32) * dp, axis=0, keepdims=True)
    ds = (p * (dp - delta)).astype(jnp.bfloat16)
    gq_ref[...] = (dot(ds, kc, 0, 0) * SCALE).astype(jnp.bfloat16)
    kt = dot(ds, q, 1, 0) * SCALE
    vt = dot(pb, g, 1, 0)

    @pl.when(h >= 2)
    def _():
        for c in sends(slot, h - 2):
            c.wait()

    for t, term in ((0, kt), (1, vt)):
        def at(j, term=term):
            return term[j * BLK:(j + 1) * BLK]

        window_ref[0, t] = at(0).astype(jnp.bfloat16)
        own_ref[0, t] = at(1)
        window_ref[1, t] = at(2).astype(jnp.bfloat16)
        sink_ref[0, t] = at(3).astype(jnp.bfloat16)
        sink_ref[1, t] = at(4).astype(jnp.bfloat16)
        for j in range(3):
            terms[slot, j, t] = at(5 + j).astype(jnp.bfloat16)
    for c in sends(slot, h):
        c.start()

    @pl.when(h == H - 1)
    def _():
        for c in sends(1 - slot, h - 1) + sends(slot, h):
            c.wait()


def attend(where, q, g, k, v, near, fetched, n, most):
    col = pl.BlockSpec((BLK, HD), lambda h, w: (0, h))

    def far(j):
        return pl.BlockSpec(
            (1, 1, 2, BLK, HD), lambda h, w: (w[3 * h + j], w[3 * H + 3 * h + j], 0, 0, 0))

    return pl.pallas_call(
        functools.partial(core_kernel, n),
        out_shape=(
            jax.ShapeDtypeStruct((BLK, WIDTH), jnp.bfloat16),
            jax.ShapeDtypeStruct((H, 2, BLK, HD), jnp.float32),
            jax.ShapeDtypeStruct((2, 2, BLK, WIDTH), jnp.bfloat16),
            jax.ShapeDtypeStruct((2, 2, BLK, WIDTH), jnp.bfloat16),
            jax.ShapeDtypeStruct((n, most, 2, BLK, HD), jnp.bfloat16),
        ),
        grid_spec=pltpu.PrefetchScalarGridSpec(
            num_scalar_prefetch=1,
            grid=(H,),
            in_specs=[col, col, col, col,
                      pl.BlockSpec((4, 2, BLK, HD), lambda h, w: (0, 0, 0, h)),
                      far(0), far(1), far(2)],
            out_specs=(
                col,
                pl.BlockSpec((1, 2, BLK, HD), lambda h, w: (h, 0, 0, 0)),
                pl.BlockSpec((2, 2, BLK, HD), lambda h, w: (0, 0, 0, h)),
                pl.BlockSpec((2, 2, BLK, HD), lambda h, w: (0, 0, 0, h)),
                ANY,
            ),
            scratch_shapes=[
                pltpu.VMEM((2, 3, 2, BLK, HD), jnp.bfloat16),
                pltpu.SemaphoreType.DMA((2, 3)),
            ],
        ),
        compiler_params=pltpu.CompilerParams(vmem_limit_bytes=48 << 20),
        cost_estimate=pl.CostEstimate(flops=3_000_000_000, bytes_accessed=24 << 20, transcendentals=2 << 20),
        name="attend",
    )(where, q, g, k, v, near, fetched, fetched, fetched)


def combine_kernel(n, most, wanted, own, halo, sinks, returned, gk_ref, gv_ref, acc):
    me = wanted[n * most]
    lower, upper, root = me > 0, me < n - 1, me < 2
    for h in range(H):
        cols = slice(h * HD, (h + 1) * HD)
        for t in range(2):
            acc[h, t] = (
                own[h, t]
                + jnp.where(lower, halo[0, t, :, cols].astype(jnp.float32), 0.0)
                + jnp.where(upper, halo[1, t, :, cols].astype(jnp.float32), 0.0)
                + jnp.where(root, sinks[t, :, cols], 0.0)
            )

    def body(i, _):
        h = wanted[i]

        @pl.when(h >= 0)
        def _():
            acc[h] += returned[i].astype(jnp.float32)

        return 0

    lax.fori_loop(0, n * most, body, 0)
    for h in range(H):
        cols = slice(h * HD, (h + 1) * HD)
        gk_ref[:, cols] = acc[h, 0].astype(jnp.bfloat16)
        gv_ref[:, cols] = acc[h, 1].astype(jnp.bfloat16)


def combine(wanted, own, halo, sinks, returned, n, most):
    out = jax.ShapeDtypeStruct((BLK, WIDTH), jnp.bfloat16)
    return pl.pallas_call(
        functools.partial(combine_kernel, n, most),
        out_shape=(out, out),
        in_specs=[SMEM, VMEM, VMEM, VMEM, VMEM],
        out_specs=(VMEM, VMEM),
        scratch_shapes=[pltpu.VMEM((H, 2, BLK, HD), jnp.float32)],
        compiler_params=pltpu.CompilerParams(vmem_limit_bytes=48 << 20),
        cost_estimate=pl.CostEstimate(flops=4_000_000, bytes_accessed=9 << 20, transcendentals=0),
        name="combine",
    )(wanted, own, halo, sinks, returned.reshape(n * most, 2, BLK, HD))


def per_device(queries, keys, values, grad_out, partners):
    n = lax.axis_size("seq")
    me = lax.axis_index("seq").astype(jnp.int32)
    most = max(2, (3 * H + n - 1) // n)
    items = 3 * H
    dests = partners.reshape(items)
    heads = jnp.arange(items, dtype=jnp.int32) // 3
    order = jnp.arange(items)
    same = (dests[:, None] == dests[None, :]) & (order[None, :] < order[:, None])
    rank = jnp.sum(same.astype(jnp.int32), axis=1)
    places = jnp.arange(n * 128, dtype=jnp.int32)
    hit = places[:, None] == (dests * 128 + rank)[None, :]
    asks = jnp.max(jnp.where(hit, heads[None, :], -1), axis=1).reshape(n, 1, 128)
    near, fetched, wanted = fetch(asks, keys, values, n, most)
    where = jnp.concatenate([dests, rank, me[None]])
    grad_queries, own, window, sinks, outbox = attend(
        where, queries, grad_out, keys, values, near, fetched, n, most)
    returned, halo, total = collect(outbox, window, sinks, n, most)
    table = jnp.concatenate([wanted[:, 0, :most].reshape(-1), me[None]])
    grad_keys, grad_values = combine(table, own, halo, total, returned, n, most)
    return grad_queries, grad_keys, grad_values


def solution(mesh):
    block = P(("groups", "seq"), None)
    return jax.shard_map(
        per_device,
        mesh=mesh,
        in_specs=(block, block, block, block, P(("groups", "seq"), None, None)),
        out_specs=(block, block, block),
        check_vma=False,
    )
```

time: 379 us -> 271 us (0.72)
  Pallas kernels: 309 us -> 259 us
  starting transfers between devices: 44 us -> 0 us
  blocking collectives: 13.6 us -> 0 us
    pallas_call x3 -> x2, Pallas kernels: 281 us -> 231 us  [the longest x1 117 us: collect(): pl.pallas_call(functools.partial(collect_kernel, n), out_shape=(jax.Shape...]
    all_to_all x2 -> x0, starting transfers between devices: 44 us -> none  [the longest x1 39.3 us: per_device(): lax.all_to_all(outbox, 'seq', split_axis=0, concat_axis=0, tiled=True)]
    all_to_all x1 -> x0, blocking collectives: 13.6 us -> none  [per_device(): lax.all_to_all(requests, 'seq', split_axis=0, concat_axis=0, tiled=True)]
    unnamed x19 -> x17, local copies, waits for them, and re-layouts: 9.08 us -> 10 us
  transfers between devices with their start and end apart: 2 -> 0, of which waited for: 0 -> 0; matrix products, arithmetic and copies ran while one was open for 0% -> 0% of each run, Pallas kernels for 49% -> 0%
where the time goes in v3:
time: 271 us; the launch traced here: 270 us
  Pallas kernels  259 us (96%)
  local copies, waits for them, and re-layouts  10.2 us (4%)
    pallas_call x1, Pallas kernels, collect(): pl.pallas_call(functools.partial(collect_kernel, n), out_shape=(jax.Shape...  117 us
    pallas_call x1, Pallas kernels, fetch(): pl.pallas_call(functools.partial(fetch_kernel, n, most), out_shape=(jax.S...  113 us
    pallas_call x1, Pallas kernels, attend(): pl.pallas_call(functools.partial(core_kernel, n), out_shape=(jax.ShapeDty...  22.7 us
    unnamed x17, local copies, waits for them, and re-layouts  10 us
    pallas_call x1, Pallas kernels, combine(): pl.pallas_call(functools.partial(combine_kernel, n, most), out_shape=(out...  5.48 us

profile of v3, /device:TPU:0, one launch (start us, length us, event | category | flops | bytes accessed | tf_op | source)
XLA Modules:
  0.0 270.4 jit_solution(14890333191078879039)
XLA Ops:
  0.6 0.8 copy.10
  1.4 0.1 reshape.38
  1.5 0.2 convert_reduce_fusion
  1.7 0.1 pad_add_fusion.where
  1.8 0.1 select_reduce_fusion
  1.9 0.0 copy-start.2
  1.9 1.0 copy-done.2
  3.0 0.0 copy-start.4
  3.0 1.0 copy-done.4
  4.0 113.4 %fetch.1 = (bf16[4,2,128,2048]{3,2,1,0:T(8,128)(2,1)}, bf16[16,3,2,128,128]{4,3,2,1,0:T(8,128)(2,1)S(1)}, s32[16,1,128]{2,1,0:T(1,128)S(1)}) custom-call(s32[16,1,128]{2,1,0:T(1,128)S(1)} %bitcast.3, bf16[128,2048]{1,0:T(8,128)(2,1)S(1)} %copy-done.2, bf16[128,2048]{1,0:T(8,128)(2,1)S(1)} %copy-done.4), custom_call_target="tpu_custom_call" | custom-call | tf_op jit(solution)/shard_map/fetch/pallas_call | solution.py:254
  117.4 0.0 copy-start
  117.4 1.7 copy-done
  119.1 0.1 reshape_squeeze.3
  119.2 0.1 pad_add_fusion.1.wanted
  119.3 0.0 copy-start.3
  119.3 1.0 copy-done.3
  120.3 0.0 copy-start.5
  120.3 1.0 copy-done.5
  121.3 0.0 copy-start.6
  121.3 1.0 copy-done.6
  122.4 0.0 copy-start.7
  122.4 1.0 copy-done.7
  123.4 22.7 %attend.1 = (bf16[128,2048]{1,0:T(8,128)(2,1)}, f32[16,2,128,128]{3,2,1,0:T(8,128)S(1)}, bf16[2,2,128,2048]{3,2,1,0:T(8,128)(2,1)}, bf16[2,2,128,2048]{3,2,1,0:T(8,128)(2,1)}, bf16[16,3,2,128,128]{4,3,2,1,0:T(8,128)(2,1)}) custom-call(s32[97]{0:T(128)S(1)} %pad_add_fusion.where, bf16[128,2048]{1,0:T(8,128)(2,1)S(1)} %copy-done.6, ...), custom_call_target="tpu_custom_call" | custom-call | flops 3000000000 | bytes 25165824 | tf_op jit(solution)/shard_map/attend/pallas_call | solution.py:466
  146.2 117.4 %collect.1 = (bf16[16,3,2,128,128]{4,3,2,1,0:T(8,128)(2,1)}, bf16[2,2,128,2048]{3,2,1,0:T(8,128)(2,1)S(1)}, f32[2,128,2048]{2,1,0:T(8,128)S(1)}) custom-call(bf16[16,3,2,128,128]{4,3,2,1,0:T(8,128)(2,1)} %get-tuple-element.21.outbox, bf16[2,2,128,2048]{3,2,1,0:T(8,128)(2,1)} %get-tuple-element.22.window, bf16[2,2,128,2048]{3,2,1,0:T(8,128)(2,1)} %get-tuple-element.23.sinks), custom_call_target="tpu_custom_call" | custom-call | tf_op jit(solution)/shard_map/collect/pallas_call | solution.py:371
  263.5 0.0 copy-start.1
  263.6 1.3 copy-done.1
  264.9 5.5 %combine.1 = (bf16[128,2048]{1,0:T(8,128)(2,1)}, bf16[128,2048]{1,0:T(8,128)(2,1)}) custom-call(s32[49]{0:T(128)S(1)} %pad_add_fusion.1.wanted, f32[16,2,128,128]{3,2,1,0:T(8,128)S(1)} %get-tuple-element.20.own, bf16[2,2,128,2048]{3,2,1,0:T(8,128)(2,1)S(1)} %get-tuple-element.24.halo, f32[2,128,2048]{2,1,0:T(8,128)} %copy-done.1, ...), custom_call_target="tpu_custom_call" | custom-call | flops 4000000 | bytes 9437184 | tf_op jit(solution)/shard_map/combine/pallas_call | solution.py:530
  (2 shorter events, 0.0 us)
Async XLA Ops:
  1.9 1.0 copy-start.2
  3.0 1.0 copy-start.4
  117.4 1.7 copy-start
  119.3 1.0 copy-start.3
  120.3 1.0 copy-start.5
  121.3 1.0 copy-start.6
  122.4 1.0 copy-start.7
  263.5 1.3 copy-start.1

commit v4 on v3

--- a/solution.py
+++ b/solution.py
@@ -15,7 +15,7 @@
 SCALE = 1.0 / math.sqrt(HD)
 STRIDE = 4
 CHUNKS = 4
-WINDOW = 3
+WINDOW = 6
 ROWS = 2 * BLK // CHUNKS
 ANY = pl.BlockSpec(memory_space=pl.ANY)
 VMEM = pl.BlockSpec(memory_space=pltpu.VMEM)
@@ -32,7 +32,8 @@
 def signs(n):
     me = lax.axis_index("seq")
     rung = me // STRIDE
-    root, side = me < 2, jnp.logical_and(me >= 2, me < STRIDE)
+    root = me < 2
+    column = lax.rem(me, STRIDE) // 2
     return dict(
         me=me,
         core=lax.rem(me, 2),
@@ -42,11 +43,11 @@
         odd=lax.rem(me, 2) == 1,
         even=lax.rem(me, 2) == 0,
         root=root,
-        side=side,
-        down=me >= STRIDE,
+        high=me >= STRIDE,
         up=me + STRIDE < n,
-        depth=rung + lax.rem(me, STRIDE) // 2,
-        height=n // STRIDE - 1 - rung + root.astype(jnp.int32),
+        rung=rung,
+        column=column,
+        across=me + 2 - 4 * column,
     )
 
 
@@ -137,7 +138,7 @@
         return remote(src, piece(near, 2 + core, i), tree_s.at[i], tree_r.at[i], me + STRIDE)
 
     def to_side(i, src):
-        return remote(src, piece(near, 2 + core, i), side_s.at[i], tree_r.at[i], me + 2)
+        return remote(src, piece(near, 2 + core, i), side_s.at[i], tree_r.at[i], r["across"])
 
     def to_sibling(i, src):
         return remote(src, piece(near, 2 + core, i), sib_s.at[i], sib_r.at[i], r["sibling"])
@@ -153,11 +154,17 @@
         return remote((keys, values)[t], near.at[slot, t], halo_s.at[slot, t], halo_r.at[slot, t],
                       me + (1 if up else -1))
 
-    def relay(i):
+    def rises(p):
+        return jnp.logical_and(r["up"], r["column"] == p)
+
+    def crosses(p):
+        return jnp.logical_or(root, jnp.logical_and(r["high"], r["column"] == p))
+
+    def relay(i, p):
         for t in range(2):
             @pl.when(jnp.logical_and(root, i // (CHUNKS // 2) == t))
             def _(t=t):
-                @pl.when(r["up"])
+                @pl.when(rises(p))
                 def _():
                     to_up(i, own(t, i)).start()
 
@@ -168,18 +175,24 @@
         def _():
             to_up(i, piece(near, 2 + core, i)).wait_recv()
 
-            @pl.when(r["up"])
+            @pl.when(rises(p))
             def _():
                 to_up(i, piece(near, 2 + core, i)).start()
 
+            @pl.when(crosses(p))
+            def _():
+                to_side(i, piece(near, 2 + core, i)).start()
+
             to_sibling(i, piece(near, 2 + core, i)).start()
 
     def relay_at(step):
-        i = step - 2 * r["depth"]
-
-        @pl.when(jnp.logical_and(i >= 0, i < CHUNKS))
-        def _():
-            relay(i)
+        for p in range(2):
+            lag = 2 * r["rung"] + (2 * r["column"] if p == 0 else 3 - r["column"])
+            i = step - jnp.where(root, 0, lag)
+
+            @pl.when(jnp.logical_and(jnp.logical_and(i >= 0, i < CHUNKS), lax.rem(i + 2 * n, 2) == p))
+            def _(i=i, p=p):
+                relay(i, p)
 
     relay_at(0)
     halo_starts(r, 0, to_halo)
@@ -232,11 +245,11 @@
         from_sibling(i).wait_recv()
         to_sibling(i, piece(near, 2 + core, i)).wait_send()
 
-        @pl.when(r["up"])
+        @pl.when(rises(i % 2))
         def _(i=i):
             to_up(i, piece(near, 2 + core, i)).wait_send()
 
-        @pl.when(root)
+        @pl.when(crosses(i % 2))
         def _(i=i):
             to_side(i, piece(near, 2 + core, i)).wait_send()
 
@@ -287,7 +300,7 @@
         return remote(tree_out.at[i], tree_in.at[i], tree_s.at[i], tree_r.at[i], me - STRIDE)
 
     def to_side(i):
-        return remote(tree_out.at[i], side_in.at[i], tree_s.at[i], side_r.at[i], me - 2)
+        return remote(tree_out.at[i], side_in.at[i], tree_s.at[i], side_r.at[i], r["across"])
 
     def to_halo(t, up):
         slot = 0 if up else 1
@@ -302,18 +315,27 @@
         peer = lax.rem(me + k, n)
         return remote(outbox.at[peer], returned.at[peer], all_s.at[peer], all_r.at[peer], peer)
 
-    def add(i):
+    def trunk(p):
+        return r["column"] == p
+
+    def falls(p):
+        return jnp.logical_and(trunk(p), r["high"])
+
+    def crosses(p):
+        return jnp.logical_not(jnp.logical_or(r["root"], falls(p)))
+
+    def add(i, p):
         half = CHUNKS // 2
         t, rows = i // half, pl.ds(pl.multiple_of(lax.rem(i, half) * ROWS, ROWS), ROWS)
         to_sibling(i).wait_recv()
         total[t, rows] = sinks[core, t, rows].astype(jnp.float32) + sib_in[i].astype(jnp.float32)
 
-        @pl.when(r["up"])
+        @pl.when(jnp.logical_and(r["up"], trunk(p)))
         def _():
             to_down(i).wait_recv()
             total[t, rows] += tree_in[i].astype(jnp.float32)
 
-        @pl.when(r["root"])
+        @pl.when(jnp.logical_or(r["root"], falls(p)))
         def _():
             to_side(i).wait_recv()
             total[t, rows] += side_in[i].astype(jnp.float32)
@@ -322,11 +344,11 @@
         def _():
             tree_out[i] = total[t, rows].astype(jnp.bfloat16)
 
-        @pl.when(r["down"])
+        @pl.when(falls(p))
         def _():
             to_down(i).start()
 
-        @pl.when(r["side"])
+        @pl.when(crosses(p))
         def _():
             to_side(i).start()
 
@@ -338,11 +360,16 @@
             send(hops[step - WINDOW]).wait_send()
         send(k).start()
         halo_starts(r, step, to_halo)
-        i = step - 2 * r["height"] - 1
-
-        @pl.when(jnp.logical_and(i >= 0, i < CHUNKS))
-        def _(i=i):
-            add(i)
+        for p in range(2):
+            top = n // STRIDE - 1
+            lag = jnp.where(trunk(p), 3 + 2 * (top - r["rung"]), 1)
+            if p == 1:
+                lag = jnp.where(r["root"], 5 + 2 * top, lag)
+            i = step - lag
+
+            @pl.when(jnp.logical_and(jnp.logical_and(i >= 0, i < CHUNKS), lax.rem(i + 2 * n, 2) == p))
+            def _(i=i, p=p):
+                add(i, p)
 
     self_copy = pltpu.make_async_copy(outbox.at[me], returned.at[me], table)
     self_copy.start()
@@ -353,11 +380,11 @@
     for i in range(CHUNKS):
         to_sibling(i).wait_send()
 
-        @pl.when(r["down"])
+        @pl.when(falls(i % 2))
         def _(i=i):
             to_down(i).wait_send()
 
-        @pl.when(r["side"])
+        @pl.when(crosses(i % 2))
         def _(i=i):
             to_side(i).wait_send()
 

time: 271 us -> 264 us (0.974)
  Pallas kernels: 259 us -> 252 us
    pallas_call x1, Pallas kernels: 117 us -> 104 us  [collect(): pl.pallas_call(functools.partial(collect_kernel, n), out_shape=(jax.Shape...]
    pallas_call x1, Pallas kernels: 113 us -> 120 us  [fetch(): pl.pallas_call(functools.partial(fetch_kernel, n, most), out_shape=(jax.S...]
where the time goes in v4:
time: 264 us
  Pallas kernels  252 us (95%)
  local copies, waits for them, and re-layouts  10.2 us (4%)
    pallas_call x1, Pallas kernels, fetch(): pl.pallas_call(functools.partial(fetch_kernel, n, most), out_shape=(jax.S...  120 us
    pallas_call x1, Pallas kernels, collect(): pl.pallas_call(functools.partial(collect_kernel, n), out_shape=(jax.Shape...  104 us
    pallas_call x1, Pallas kernels, attend(): pl.pallas_call(functools.partial(core_kernel, n), out_shape=(jax.ShapeDty...  22.7 us
    unnamed x17, local copies, waits for them, and re-layouts  10 us
    pallas_call x1, Pallas kernels, combine(): pl.pallas_call(functools.partial(combine_kernel, n, most), out_shape=(out...  5.48 us

profile of v4, /device:TPU:0, one launch (start us, length us, event | category | flops | bytes accessed | tf_op | source)
XLA Modules:
  0.0 263.7 jit_solution(13157153265018501954)
XLA Ops:
  0.6 0.8 copy.10
  1.4 0.1 reshape.38
  1.5 0.2 convert_reduce_fusion
  1.7 0.1 pad_add_fusion.where
  1.8 0.1 select_reduce_fusion
  1.9 0.0 copy-start.2
  1.9 1.0 copy-done.2
  3.0 0.0 copy-start.4
  3.0 1.0 copy-done.4
  4.0 119.8 %fetch.1 = (bf16[4,2,128,2048]{3,2,1,0:T(8,128)(2,1)}, bf16[16,3,2,128,128]{4,3,2,1,0:T(8,128)(2,1)S(1)}, s32[16,1,128]{2,1,0:T(1,128)S(1)}) custom-call(s32[16,1,128]{2,1,0:T(1,128)S(1)} %bitcast.3, bf16[128,2048]{1,0:T(8,128)(2,1)S(1)} %copy-done.2, bf16[128,2048]{1,0:T(8,128)(2,1)S(1)} %copy-done.4), custom_call_target="tpu_custom_call" | custom-call | tf_op jit(solution)/shard_map/fetch/pallas_call | solution.py:267
  123.9 0.0 copy-start
  123.9 1.7 copy-done
  125.6 0.1 reshape_squeeze.3
  125.7 0.1 pad_add_fusion.1.wanted
  125.7 0.0 copy-start.3
  125.8 1.0 copy-done.3
  126.8 0.0 copy-start.5
  126.8 1.0 copy-done.5
  127.8 0.0 copy-start.6
  127.8 1.0 copy-done.6
  128.9 0.0 copy-start.7
  128.9 1.0 copy-done.7
  129.9 22.7 %attend.1 = (bf16[128,2048]{1,0:T(8,128)(2,1)}, f32[16,2,128,128]{3,2,1,0:T(8,128)S(1)}, bf16[2,2,128,2048]{3,2,1,0:T(8,128)(2,1)}, bf16[2,2,128,2048]{3,2,1,0:T(8,128)(2,1)}, bf16[16,3,2,128,128]{4,3,2,1,0:T(8,128)(2,1)}) custom-call(s32[97]{0:T(128)S(1)} %pad_add_fusion.where, bf16[128,2048]{1,0:T(8,128)(2,1)S(1)} %copy-done.6, ...), custom_call_target="tpu_custom_call" | custom-call | flops 3000000000 | bytes 25165824 | tf_op jit(solution)/shard_map/attend/pallas_call | solution.py:493
  152.6 104.2 %collect.1 = (bf16[16,3,2,128,128]{4,3,2,1,0:T(8,128)(2,1)}, bf16[2,2,128,2048]{3,2,1,0:T(8,128)(2,1)S(1)}, f32[2,128,2048]{2,1,0:T(8,128)S(1)}) custom-call(bf16[16,3,2,128,128]{4,3,2,1,0:T(8,128)(2,1)} %get-tuple-element.21.outbox, bf16[2,2,128,2048]{3,2,1,0:T(8,128)(2,1)} %get-tuple-element.22.window, bf16[2,2,128,2048]{3,2,1,0:T(8,128)(2,1)} %get-tuple-element.23.sinks), custom_call_target="tpu_custom_call" | custom-call | tf_op jit(solution)/shard_map/collect/pallas_call | solution.py:398
  256.8 0.0 copy-start.1
  256.9 1.3 copy-done.1
  258.2 5.5 %combine.1 = (bf16[128,2048]{1,0:T(8,128)(2,1)}, bf16[128,2048]{1,0:T(8,128)(2,1)}) custom-call(s32[49]{0:T(128)S(1)} %pad_add_fusion.1.wanted, f32[16,2,128,128]{3,2,1,0:T(8,128)S(1)} %get-tuple-element.20.own, bf16[2,2,128,2048]{3,2,1,0:T(8,128)(2,1)S(1)} %get-tuple-element.24.halo, f32[2,128,2048]{2,1,0:T(8,128)} %copy-done.1, ...), custom_call_target="tpu_custom_call" | custom-call | flops 4000000 | bytes 9437184 | tf_op jit(solution)/shard_map/combine/pallas_call | solution.py:557
  (2 shorter events, 0.0 us)
Async XLA Ops:
  1.9 1.0 copy-start.2
  3.0 1.0 copy-start.4
  123.9 1.7 copy-start
  125.7 1.0 copy-start.3
  126.8 1.0 copy-start.5
  127.8 1.0 copy-start.6
  128.9 1.0 copy-start.7
  256.8 1.3 copy-start.1

commit v5 on v4

--- a/solution.py
+++ b/solution.py
@@ -282,7 +282,7 @@
             dma((2, 2)), dma((2, 2)),
         ],
         compiler_params=pltpu.CompilerParams(
-            collective_id=0, has_side_effects=True, vmem_limit_bytes=48 << 20),
+            collective_id=0, has_side_effects=True, vmem_limit_bytes=60 << 20),
         name="fetch",
     )(asks, keys, values)
 
@@ -406,7 +406,7 @@
         out_specs=(ANY, ANY, VMEM),
         scratch_shapes=[part] * 4 + [dma, dma((n,)), dma((n,))] + [dma((CHUNKS,))] * 5 + [dma((2, 2))] * 2,
         compiler_params=pltpu.CompilerParams(
-            collective_id=1, has_side_effects=True, vmem_limit_bytes=48 << 20),
+            collective_id=1, has_side_effects=True, vmem_limit_bytes=60 << 20),
         name="collect",
     )(outbox, window, sinks)
 
@@ -517,7 +517,7 @@
                 pltpu.SemaphoreType.DMA((2, 3)),
             ],
         ),
-        compiler_params=pltpu.CompilerParams(vmem_limit_bytes=48 << 20),
+        compiler_params=pltpu.CompilerParams(vmem_limit_bytes=60 << 20),
         cost_estimate=pl.CostEstimate(flops=3_000_000_000, bytes_accessed=24 << 20, transcendentals=2 << 20),
         name="attend",
     )(where, q, g, k, v, near, fetched, fetched, fetched)
@@ -560,7 +560,7 @@
         in_specs=[SMEM, VMEM, VMEM, VMEM, VMEM],
         out_specs=(VMEM, VMEM),
         scratch_shapes=[pltpu.VMEM((H, 2, BLK, HD), jnp.float32)],
-        compiler_params=pltpu.CompilerParams(vmem_limit_bytes=48 << 20),
+        compiler_params=pltpu.CompilerParams(vmem_limit_bytes=60 << 20),
         cost_estimate=pl.CostEstimate(flops=4_000_000, bytes_accessed=9 << 20, transcendentals=0),
         name="combine",
     )(wanted, own, halo, sinks, returned.reshape(n * most, 2, BLK, HD))

time: 264 us -> 261 us (0.989)
  local copies, waits for them, and re-layouts: 10.2 us -> 1.65 us
  Pallas kernels: 252 us -> 256 us
    unnamed x17 -> x1, local copies, waits for them, and re-layouts: 10 us -> 0.76 us
where the time goes in v5:
time: 261 us
  Pallas kernels  256 us (98%)
    pallas_call x1, Pallas kernels, fetch(): pl.pallas_call(functools.partial(fetch_kernel, n, most), out_shape=(jax.S...  121 us
    pallas_call x1, Pallas kernels, collect(): pl.pallas_call(functools.partial(collect_kernel, n), out_shape=(jax.Shape...  106 us
    pallas_call x1, Pallas kernels, attend(): pl.pallas_call(functools.partial(core_kernel, n), out_shape=(jax.ShapeDty...  22.5 us
    pallas_call x1, Pallas kernels, combine(): pl.pallas_call(functools.partial(combine_kernel, n, most), out_shape=(out...  6.65 us

profile of v5, /device:TPU:0, one launch (start us, length us, event | category | flops | bytes accessed | tf_op | source)
XLA Modules:
  0.0 260.7 jit_solution(8676291684049661790)
XLA Ops:
  0.6 0.8 copy.10
  1.4 0.1 reshape.38
  1.5 0.2 convert_reduce_fusion
  1.7 0.7 pad_add_fusion.where
  2.3 0.7 select_reduce_fusion
  3.1 121.2 %fetch.1 = (bf16[4,2,128,2048]{3,2,1,0:T(8,128)(2,1)}, bf16[16,3,2,128,128]{4,3,2,1,0:T(8,128)(2,1)}, s32[16,1,128]{2,1,0:T(1,128)}) custom-call(s32[16,1,128]{2,1,0:T(1,128)} %bitcast.4, bf16[128,2048]{1,0:T(8,128)(2,1)} %k_ref.1, bf16[128,2048]{1,0:T(8,128)(2,1)} %v_ref.1), custom_call_target="tpu_custom_call" | custom-call | tf_op jit(solution)/shard_map/fetch/pallas_call | solution.py:267
  124.3 0.7 slice_reduce_fusion
  125.0 0.1 reshape_squeeze.3
  125.1 0.7 pad_add_fusion.1.wanted
  125.8 22.5 %attend.1 = (bf16[128,2048]{1,0:T(8,128)(2,1)}, f32[16,2,128,128]{3,2,1,0:T(8,128)}, bf16[2,2,128,2048]{3,2,1,0:T(8,128)(2,1)}, bf16[2,2,128,2048]{3,2,1,0:T(8,128)(2,1)}, bf16[16,3,2,128,128]{4,3,2,1,0:T(8,128)(2,1)}) custom-call(s32[97]{0:T(128)} %pad_add_fusion.where, bf16[128,2048]{1,0:T(8,128)(2,1)} %q_ref.1, bf16[128,2048]{1,0:T(8,128)(2,1)} %g_ref.1, ...), custom_call_target="tpu_custom_call" | custom-call | flops 3000000000 | bytes 25165824 | tf_op jit(solution)/shard_map/attend/pallas_call | solution.py:493
  148.3 105.7 %collect.1 = (bf16[16,3,2,128,128]{4,3,2,1,0:T(8,128)(2,1)}, bf16[2,2,128,2048]{3,2,1,0:T(8,128)(2,1)}, f32[2,128,2048]{2,1,0:T(8,128)}) custom-call(bf16[16,3,2,128,128]{4,3,2,1,0:T(8,128)(2,1)} %get-tuple-element.21.outbox, bf16[2,2,128,2048]{3,2,1,0:T(8,128)(2,1)} %get-tuple-element.22.window, bf16[2,2,128,2048]{3,2,1,0:T(8,128)(2,1)} %get-tuple-element.23.sinks), custom_call_target="tpu_custom_call" | custom-call | tf_op jit(solution)/shard_map/collect/pallas_call | solution.py:398
  254.0 6.7 %combine.1 = (bf16[128,2048]{1,0:T(8,128)(2,1)}, bf16[128,2048]{1,0:T(8,128)(2,1)}) custom-call(s32[49]{0:T(128)} %pad_add_fusion.1.wanted, f32[16,2,128,128]{3,2,1,0:T(8,128)} %get-tuple-element.20.own, bf16[2,2,128,2048]{3,2,1,0:T(8,128)(2,1)} %get-tuple-element.24.halo, f32[2,128,2048]{2,1,0:T(8,128)} %get-tuple-element.25.sinks, ...), custom_call_target="tpu_custom_call" | custom-call | flops 4000000 | bytes 9437184 | tf_op jit(solution)/shard_map/combine/pallas_call | solution.py:557
  (1 shorter events, 0.0 us)
